TPU v7x, 256 devices: a whole 4x4x8 slice. The times are simulated.
256 devices in a mesh: row: 32 (over x, z), feat: 8 (over y, core).
Axes of the slice: x: 4, y: 4, z: 8, core: 2. Of those that a mesh axis runs over, the one named last changes fastest.
Arguments:
- scores: float32 [192, 1024], P('row'), may hold values from -8 to 8, as said below
- labels: int32 [192, 1024], P('row'), may hold values from 0 to 4
- counts: int32 [192], P('row'), may hold values from 1 to 1024, 147456 in all
- bin_codes: int32 [192, 768, 1024], P('row', 'feat'), may hold values from 0 to 255
- row_child: int32 [192, 1024], P('row'), may hold values from 0 to 15
- smaller: int32 [8], replicated, may hold values from 0 to 1, as said below
- parent_hist: float32 [256, 8, 1536], P('row', None, 'feat'), may hold values from -10 to 10
Outputs:
- children: float32 [256, 8, 3072], P('row', None, 'feat')
- best_gain: float32 [8], replicated
Inputs may be any that keep to these rules, and one draw needn't show every extreme that they name: Each query's scores never rise from one slot to the next. The counts of all queries sum to 147456, and some query is full. `smaller`: exactly half of the 8 parents have the value 1.
All inputs are finite; a program needn't handle non-finite values. No bound on the sum of `counts` on one device may be relied on, other than what follows from the above.
Results may differ from a plain program's by a relative error of at most 0.0028.
Values may be sent and summed in bfloat16 or wider, within the bound.
No kernel may reach another device: no remote copies, remote signals or barrier semaphores. Data moves between devices by JAX's collectives and lax.ppermute only.
A program may use at most 64 MiB of HBM per device.

v0:
```python
import math

import jax
import jax.numpy as jnp
from jax import lax
from jax.sharding import PartitionSpec as P

levels = 5
reg_lambda = 1.0


def query_terms(labels, counts):
    slot_count = labels.shape[1]
    position = jnp.arange(slot_count, dtype=jnp.int32)
    usable = position[None, :] < counts[:, None]
    grades = jnp.arange(levels, dtype=jnp.int32)
    same_grade = labels[:, :, None] == grades[None, None, :]
    label_hot = (same_grade & usable[:, :, None]).astype(jnp.int32)
    per_grade = jnp.sum(label_hot, axis=1)
    above_count = jnp.sum(
        per_grade[:, None, :] * (grades[None, None, :] > labels[:, :, None]).astype(jnp.int32),
        axis=2,
    )
    running = jnp.cumsum(label_hot, axis=1) - label_hot
    before_count = jnp.sum(running * same_grade.astype(jnp.int32), axis=2)
    ideal_rank = above_count + before_count
    rel_gain = jnp.exp2(labels.astype(jnp.float32)) - 1.0
    discount = 1.0 / jnp.log2(position.astype(jnp.float32) + 2.0)
    ideal_terms = jnp.where(usable, rel_gain / jnp.log2(ideal_rank.astype(jnp.float32) + 2.0), 0.0)
    inv_ideal = 1.0 / jnp.maximum(jnp.sum(ideal_terms, axis=1), 1.0)
    return (usable, rel_gain, discount, inv_ideal)


def pair_block(
    row_scores,
    row_labels,
    row_gain,
    row_disc,
    row_usable,
    scores,
    labels,
    rel_gain,
    discount,
    usable,
    inv_ideal,
):
    score_gap = row_scores[:, :, None] - scores[:, None, :]
    higher = row_labels[:, :, None] > labels[:, None, :]
    live_pair = (
        (row_labels[:, :, None] != labels[:, None, :]) & row_usable[:, :, None] & usable[:, None, :]
    )
    pair_sign = jnp.where(higher, 1.0, -1.0)
    pair_prob = jax.nn.sigmoid(-pair_sign * score_gap)
    pair_weight = (
        jnp.abs(row_gain[:, :, None] - rel_gain[:, None, :])
        * jnp.abs(row_disc[None, :, None] - discount[None, None, :])
        * inv_ideal[:, None, None]
    )
    lam_grad = -jnp.sum(jnp.where(live_pair, pair_sign * pair_prob * pair_weight, 0.0), axis=2)
    lam_hess = jnp.sum(
        jnp.where(live_pair, pair_prob * (1.0 - pair_prob) * pair_weight, 0.0), axis=2
    )
    return (lam_grad, lam_hess)


def node_weights(lam_g16, lam_h16, row_child, smaller):
    parents = smaller.shape[0]
    built_node = 2 * jnp.arange(parents, dtype=jnp.int32) + smaller
    member = (row_child[:, :, None] == built_node[None, None, :]).astype(jnp.bfloat16)
    stats = jnp.stack((lam_g16, lam_h16), axis=-1)
    weights = member[:, :, :, None] * stats[:, :, None, :]
    return weights.reshape(row_child.shape[0], row_child.shape[1], parents * 2)


def split_gain(left_sums, totals):
    grad_left = left_sums[..., 0]
    hess_left = left_sums[..., 1]
    grad_total = totals[..., 0]
    hess_total = totals[..., 1]
    grad_right = grad_total - grad_left
    return (
        grad_left * grad_left / (hess_left + reg_lambda)
        + grad_right * grad_right / (hess_total - hess_left + reg_lambda)
        - grad_total * grad_total / (hess_total + reg_lambda)
    )


def bin_histogram(bin_codes, weights, number):
    feat_dev = bin_codes.shape[1]
    node_cols = weights.shape[2]
    feat_block = math.gcd(feat_dev, 4)
    bin_marks = jnp.arange(number, dtype=jnp.int32)

    def one_block(first_feat):
        code_block = lax.dynamic_slice_in_dim(bin_codes, first_feat, feat_block, 1)
        one_hot = (code_block[..., None] == bin_marks).astype(jnp.bfloat16)
        return jnp.einsum("qfnb,qnk->bfk", one_hot, weights, preferred_element_type=jnp.float32)

    pieces = lax.map(one_block, jnp.arange(feat_dev // feat_block, dtype=jnp.int32) * feat_block)
    pieces = jnp.transpose(pieces, (1, 0, 2, 3)).reshape(number, feat_dev, node_cols // 2, 2)
    return jnp.transpose(pieces, (0, 2, 1, 3)).reshape(number, node_cols // 2, feat_dev * 2)


def shards(scores, labels, counts, bin_codes, row_child, smaller, parent_hist):
    query_dev, slot_count = scores.shape
    feat_count = lax.axis_size("feat")
    row_span = slot_count // feat_count
    usable, rel_gain, discount, inv_ideal = query_terms(labels, counts)

    def block_terms(offset):

        def rows_of(array):
            return lax.dynamic_slice_in_dim(array, offset, row_span, 1)

        return pair_block(
            rows_of(scores),
            rows_of(labels),
            rows_of(rel_gain),
            lax.dynamic_slice_in_dim(discount, offset, row_span, 0),
            rows_of(usable),
            scores,
            labels,
            rel_gain,
            discount,
            usable,
            inv_ideal,
        )

    every_grad, every_hess = lax.map(
        block_terms, jnp.arange(feat_count, dtype=jnp.int32) * row_span
    )
    lam_g16 = (
        jnp.transpose(every_grad, (1, 0, 2)).reshape(query_dev, slot_count).astype(jnp.bfloat16)
    )
    lam_h16 = (
        jnp.transpose(every_hess, (1, 0, 2)).reshape(query_dev, slot_count).astype(jnp.bfloat16)
    )
    weights = node_weights(lam_g16, lam_h16, row_child, smaller)
    parents = smaller.shape[0]
    feat_dev = bin_codes.shape[1]
    bin_span = parent_hist.shape[0]
    bin_total = bin_span * lax.axis_size("row")
    all_bins = lax.psum(bin_histogram(bin_codes, weights, bin_total), "row")
    stacked_all = all_bins.reshape(bin_total, parents, feat_dev, 2)
    left_sums = jnp.cumsum(stacked_all, axis=0)
    totals = jnp.sum(stacked_all, axis=0)
    gains = split_gain(left_sums[:-1], totals[None])
    best_gain = lax.pmax(jnp.max(gains, axis=(0, 2)), "feat")
    own_bins = lax.dynamic_slice_in_dim(all_bins, lax.axis_index("row") * bin_span, bin_span, 0)
    built = own_bins.reshape(bin_span, parents, feat_dev, 2)
    sibling = parent_hist.reshape(bin_span, parents, feat_dev, 2) - built
    chosen = smaller[:, None] == jnp.arange(2, dtype=jnp.int32)[None, :]
    children = jnp.where(
        chosen[None, :, None, :, None], built[:, :, :, None, :], sibling[:, :, :, None, :]
    )
    return (children.reshape(bin_span, parents, feat_dev * 4), best_gain)


def solution(mesh):
    placed = (
        P("row", None),
        P("row", None),
        P("row"),
        P("row", "feat", None),
        P("row", None),
        P(),
        P("row", None, "feat"),
    )
    return jax.shard_map(
        shards, mesh=mesh, in_specs=placed, out_specs=(P("row", None, "feat"), P()), check_vma=False
    )
```

profile of v0, /device:TPU:1, one launch (start us, length us, event | category | flops | bytes accessed | tf_op | source)
XLA Modules:
  0.0 608.6 jit_solution(1435842050585580470)
XLA Ops:
  10.2 8.5 %reduce-window.14 = s32[6,5,8,128]{3,2,1,0:T(8,128)S(1)} reduce-window(s32[6,5,8,128]{3,2,1,0:T(8,128)S(1)} %fusion.23, s32[]{:T(128)} %constant.14.clone.1), window={size=1x1x1x128 pad=0_0x0_0x0_0x127_0}, to_apply=%region_2.0 | reduce-window | flops 3901440 | bytes 245764 | tf_op jit(solution)/shard_map/reduce-window
  22.8 72.7 %while.24 = (s32[]{:T(128)}, bf16[8,6,128]{2,1,0:T(8,128)(2,1)S(1)}, bf16[8,6,128]{2,1,0:T(8,128)(2,1)S(1)}, s32[8]{0:T(128)S(1)}, s32[6,1024]{1,0:T(8,128)}, /*...) while((s32[]{:T(128)}, ...), condition=%wide.region_9.10_spmd.clone, body=%wide.region_6.9_spmd.clone.sunk | while | flops 19135748 | bytes 1181155 | solution.py:129
  27.4 4.5 fusion.31
  36.4 4.5 fusion.31
  45.5 4.5 fusion.31
  54.6 4.5 fusion.31
  63.7 4.5 fusion.31
  72.8 4.5 fusion.31
  81.9 4.5 fusion.31
  91.0 4.5 fusion.31
  95.7 302.4 %while.25 = (s32[]{:T(128)}, f32[24,256,4,16]{1,3,2,0:T(8,128)S(1)}, s32[24]{0:T(128)S(1)}, s32[6,96,1024]{2,1,0:T(8,128)}, bf16[6,1024,2]{1,2,0:T(2,128)(2,1)S(...) while((s32[]{:T(128)}, f32[24,256,4,16]{1,3,2,0:T(8,128)S(1)}, ...), condition=%wide.region_11.12_spmd.clone, body=%wide.region_10.11_spmd.clone.sunk | while | flops 207716352 | bytes 1499291 | solution.py:99
  98.2 1.0 constant_dynamic-slice_fusion.13
  99.6 8.6 %fusion.33 = f32[24,256,4,16]{1,3,2,0:T(8,128)S(1)} fusion(f32[24,256,4,16]{1,3,2,0:T(8,128)S(1)} %get-tuple-element.361, s32[]{:T(128)S(6)} %copy.91, bf16[6,1024,16,1]{1,2,0,3:T(8,128)(2,1)S(1)} %reshape.218, s32[6,4,1024]{2,0,1:T(8,128)S(1)} %copy.76), kind=kOutput, calls=%fused_computation.29.clone.1 | convolution fusion | flops 207618048 | bytes 393220 | tf_op jit(solution)/shard_map/while/body/eval_jaxpr/qfnb,qnk->bfk/dot_general | solution.py:97
  112.2 8.6 %fusion.33 = f32[24,256,4,16]{1,3,2,0:T(8,128)S(1)} fusion(f32[24,256,4,16]{1,3,2,0:T(8,128)S(1)} %get-tuple-element.361, s32[]{:T(128)S(6)} %copy.91, bf16[6,1024,16,1]{1,2,0,3:T(8,128)(2,1)S(1)} %reshape.218, s32[6,4,1024]{2,0,1:T(8,128)S(1)} %copy.76), kind=kOutput, calls=%fused_computation.29.clone.1 | convolution fusion | flops 207618048 | bytes 393220 | tf_op jit(solution)/shard_map/while/body/eval_jaxpr/qfnb,qnk->bfk/dot_general | solution.py:97
  123.4 1.0 constant_dynamic-slice_fusion.13
  124.8 8.6 %fusion.33 = f32[24,256,4,16]{1,3,2,0:T(8,128)S(1)} fusion(f32[24,256,4,16]{1,3,2,0:T(8,128)S(1)} %get-tuple-element.361, s32[]{:T(128)S(6)} %copy.91, bf16[6,1024,16,1]{1,2,0,3:T(8,128)(2,1)S(1)} %reshape.218, s32[6,4,1024]{2,0,1:T(8,128)S(1)} %copy.76), kind=kOutput, calls=%fused_computation.29.clone.1 | convolution fusion | flops 207618048 | bytes 393220 | tf_op jit(solution)/shard_map/while/body/eval_jaxpr/qfnb,qnk->bfk/dot_general | solution.py:97
  137.4 8.6 %fusion.33 = f32[24,256,4,16]{1,3,2,0:T(8,128)S(1)} fusion(f32[24,256,4,16]{1,3,2,0:T(8,128)S(1)} %get-tuple-element.361, s32[]{:T(128)S(6)} %copy.91, bf16[6,1024,16,1]{1,2,0,3:T(8,128)(2,1)S(1)} %reshape.218, s32[6,4,1024]{2,0,1:T(8,128)S(1)} %copy.76), kind=kOutput, calls=%fused_computation.29.clone.1 | convolution fusion | flops 207618048 | bytes 393220 | tf_op jit(solution)/shard_map/while/body/eval_jaxpr/qfnb,qnk->bfk/dot_general | solution.py:97
  150.0 8.6 %fusion.33 = f32[24,256,4,16]{1,3,2,0:T(8,128)S(1)} fusion(f32[24,256,4,16]{1,3,2,0:T(8,128)S(1)} %get-tuple-element.361, s32[]{:T(128)S(6)} %copy.91, bf16[6,1024,16,1]{1,2,0,3:T(8,128)(2,1)S(1)} %reshape.218, s32[6,4,1024]{2,0,1:T(8,128)S(1)} %copy.76), kind=kOutput, calls=%fused_computation.29.clone.1 | convolution fusion | flops 207618048 | bytes 393220 | tf_op jit(solution)/shard_map/while/body/eval_jaxpr/qfnb,qnk->bfk/dot_general | solution.py:97
  162.6 8.6 %fusion.33 = f32[24,256,4,16]{1,3,2,0:T(8,128)S(1)} fusion(f32[24,256,4,16]{1,3,2,0:T(8,128)S(1)} %get-tuple-element.361, s32[]{:T(128)S(6)} %copy.91, bf16[6,1024,16,1]{1,2,0,3:T(8,128)(2,1)S(1)} %reshape.218, s32[6,4,1024]{2,0,1:T(8,128)S(1)} %copy.76), kind=kOutput, calls=%fused_computation.29.clone.1 | convolution fusion | flops 207618048 | bytes 393220 | tf_op jit(solution)/shard_map/while/body/eval_jaxpr/qfnb,qnk->bfk/dot_general | solution.py:97
  175.3 8.6 %fusion.33 = f32[24,256,4,16]{1,3,2,0:T(8,128)S(1)} fusion(f32[24,256,4,16]{1,3,2,0:T(8,128)S(1)} %get-tuple-element.361, s32[]{:T(128)S(6)} %copy.91, bf16[6,1024,16,1]{1,2,0,3:T(8,128)(2,1)S(1)} %reshape.218, s32[6,4,1024]{2,0,1:T(8,128)S(1)} %copy.76), kind=kOutput, calls=%fused_computation.29.clone.1 | convolution fusion | flops 207618048 | bytes 393220 | tf_op jit(solution)/shard_map/while/body/eval_jaxpr/qfnb,qnk->bfk/dot_general | solution.py:97
  187.9 8.6 %fusion.33 = f32[24,256,4,16]{1,3,2,0:T(8,128)S(1)} fusion(f32[24,256,4,16]{1,3,2,0:T(8,128)S(1)} %get-tuple-element.361, s32[]{:T(128)S(6)} %copy.91, bf16[6,1024,16,1]{1,2,0,3:T(8,128)(2,1)S(1)} %reshape.218, s32[6,4,1024]{2,0,1:T(8,128)S(1)} %copy.76), kind=kOutput, calls=%fused_computation.29.clone.1 | convolution fusion | flops 207618048 | bytes 393220 | tf_op jit(solution)/shard_map/while/body/eval_jaxpr/qfnb,qnk->bfk/dot_general | solution.py:97
  200.5 8.6 %fusion.33 = f32[24,256,4,16]{1,3,2,0:T(8,128)S(1)} fusion(f32[24,256,4,16]{1,3,2,0:T(8,128)S(1)} %get-tuple-element.361, s32[]{:T(128)S(6)} %copy.91, bf16[6,1024,16,1]{1,2,0,3:T(8,128)(2,1)S(1)} %reshape.218, s32[6,4,1024]{2,0,1:T(8,128)S(1)} %copy.76), kind=kOutput, calls=%fused_computation.29.clone.1 | convolution fusion | flops 207618048 | bytes 393220 | tf_op jit(solution)/shard_map/while/body/eval_jaxpr/qfnb,qnk->bfk/dot_general | solution.py:97
  213.1 8.6 %fusion.33 = f32[24,256,4,16]{1,3,2,0:T(8,128)S(1)} fusion(f32[24,256,4,16]{1,3,2,0:T(8,128)S(1)} %get-tuple-element.361, s32[]{:T(128)S(6)} %copy.91, bf16[6,1024,16,1]{1,2,0,3:T(8,128)(2,1)S(1)} %reshape.218, s32[6,4,1024]{2,0,1:T(8,128)S(1)} %copy.76), kind=kOutput, calls=%fused_computation.29.clone.1 | convolution fusion | flops 207618048 | bytes 393220 | tf_op jit(solution)/shard_map/while/body/eval_jaxpr/qfnb,qnk->bfk/dot_general | solution.py:97
  225.7 8.6 %fusion.33 = f32[24,256,4,16]{1,3,2,0:T(8,128)S(1)} fusion(f32[24,256,4,16]{1,3,2,0:T(8,128)S(1)} %get-tuple-element.361, s32[]{:T(128)S(6)} %copy.91, bf16[6,1024,16,1]{1,2,0,3:T(8,128)(2,1)S(1)} %reshape.218, s32[6,4,1024]{2,0,1:T(8,128)S(1)} %copy.76), kind=kOutput, calls=%fused_computation.29.clone.1 | convolution fusion | flops 207618048 | bytes 393220 | tf_op jit(solution)/shard_map/while/body/eval_jaxpr/qfnb,qnk->bfk/dot_general | solution.py:97
  238.3 8.6 %fusion.33 = f32[24,256,4,16]{1,3,2,0:T(8,128)S(1)} fusion(f32[24,256,4,16]{1,3,2,0:T(8,128)S(1)} %get-tuple-element.361, s32[]{:T(128)S(6)} %copy.91, bf16[6,1024,16,1]{1,2,0,3:T(8,128)(2,1)S(1)} %reshape.218, s32[6,4,1024]{2,0,1:T(8,128)S(1)} %copy.76), kind=kOutput, calls=%fused_computation.29.clone.1 | convolution fusion | flops 207618048 | bytes 393220 | tf_op jit(solution)/shard_map/while/body/eval_jaxpr/qfnb,qnk->bfk/dot_general | solution.py:97
  250.9 8.6 %fusion.33 = f32[24,256,4,16]{1,3,2,0:T(8,128)S(1)} fusion(f32[24,256,4,16]{1,3,2,0:T(8,128)S(1)} %get-tuple-element.361, s32[]{:T(128)S(6)} %copy.91, bf16[6,1024,16,1]{1,2,0,3:T(8,128)(2,1)S(1)} %reshape.218, s32[6,4,1024]{2,0,1:T(8,128)S(1)} %copy.76), kind=kOutput, calls=%fused_computation.29.clone.1 | convolution fusion | flops 207618048 | bytes 393220 | tf_op jit(solution)/shard_map/while/body/eval_jaxpr/qfnb,qnk->bfk/dot_general | solution.py:97
  263.5 8.6 %fusion.33 = f32[24,256,4,16]{1,3,2,0:T(8,128)S(1)} fusion(f32[24,256,4,16]{1,3,2,0:T(8,128)S(1)} %get-tuple-element.361, s32[]{:T(128)S(6)} %copy.91, bf16[6,1024,16,1]{1,2,0,3:T(8,128)(2,1)S(1)} %reshape.218, s32[6,4,1024]{2,0,1:T(8,128)S(1)} %copy.76), kind=kOutput, calls=%fused_computation.29.clone.1 | convolution fusion | flops 207618048 | bytes 393220 | tf_op jit(solution)/shard_map/while/body/eval_jaxpr/qfnb,qnk->bfk/dot_general | solution.py:97
  276.1 8.6 %fusion.33 = f32[24,256,4,16]{1,3,2,0:T(8,128)S(1)} fusion(f32[24,256,4,16]{1,3,2,0:T(8,128)S(1)} %get-tuple-element.361, s32[]{:T(128)S(6)} %copy.91, bf16[6,1024,16,1]{1,2,0,3:T(8,128)(2,1)S(1)} %reshape.218, s32[6,4,1024]{2,0,1:T(8,128)S(1)} %copy.76), kind=kOutput, calls=%fused_computation.29.clone.1 | convolution fusion | flops 207618048 | bytes 393220 | tf_op jit(solution)/shard_map/while/body/eval_jaxpr/qfnb,qnk->bfk/dot_general | solution.py:97
  288.7 8.6 %fusion.33 = f32[24,256,4,16]{1,3,2,0:T(8,128)S(1)} fusion(f32[24,256,4,16]{1,3,2,0:T(8,128)S(1)} %get-tuple-element.361, s32[]{:T(128)S(6)} %copy.91, bf16[6,1024,16,1]{1,2,0,3:T(8,128)(2,1)S(1)} %reshape.218, s32[6,4,1024]{2,0,1:T(8,128)S(1)} %copy.76), kind=kOutput, calls=%fused_computation.29.clone.1 | convolution fusion | flops 207618048 | bytes 393220 | tf_op jit(solution)/shard_map/while/body/eval_jaxpr/qfnb,qnk->bfk/dot_general | solution.py:97
  301.3 8.6 %fusion.33 = f32[24,256,4,16]{1,3,2,0:T(8,128)S(1)} fusion(f32[24,256,4,16]{1,3,2,0:T(8,128)S(1)} %get-tuple-element.361, s32[]{:T(128)S(6)} %copy.91, bf16[6,1024,16,1]{1,2,0,3:T(8,128)(2,1)S(1)} %reshape.218, s32[6,4,1024]{2,0,1:T(8,128)S(1)} %copy.76), kind=kOutput, calls=%fused_computation.29.clone.1 | convolution fusion | flops 207618048 | bytes 393220 | tf_op jit(solution)/shard_map/while/body/eval_jaxpr/qfnb,qnk->bfk/dot_general | solution.py:97
  313.9 8.6 %fusion.33 = f32[24,256,4,16]{1,3,2,0:T(8,128)S(1)} fusion(f32[24,256,4,16]{1,3,2,0:T(8,128)S(1)} %get-tuple-element.361, s32[]{:T(128)S(6)} %copy.91, bf16[6,1024,16,1]{1,2,0,3:T(8,128)(2,1)S(1)} %reshape.218, s32[6,4,1024]{2,0,1:T(8,128)S(1)} %copy.76), kind=kOutput, calls=%fused_computation.29.clone.1 | convolution fusion | flops 207618048 | bytes 393220 | tf_op jit(solution)/shard_map/while/body/eval_jaxpr/qfnb,qnk->bfk/dot_general | solution.py:97
  326.5 8.6 %fusion.33 = f32[24,256,4,16]{1,3,2,0:T(8,128)S(1)} fusion(f32[24,256,4,16]{1,3,2,0:T(8,128)S(1)} %get-tuple-element.361, s32[]{:T(128)S(6)} %copy.91, bf16[6,1024,16,1]{1,2,0,3:T(8,128)(2,1)S(1)} %reshape.218, s32[6,4,1024]{2,0,1:T(8,128)S(1)} %copy.76), kind=kOutput, calls=%fused_computation.29.clone.1 | convolution fusion | flops 207618048 | bytes 393220 | tf_op jit(solution)/shard_map/while/body/eval_jaxpr/qfnb,qnk->bfk/dot_general | solution.py:97
  339.1 8.6 %fusion.33 = f32[24,256,4,16]{1,3,2,0:T(8,128)S(1)} fusion(f32[24,256,4,16]{1,3,2,0:T(8,128)S(1)} %get-tuple-element.361, s32[]{:T(128)S(6)} %copy.91, bf16[6,1024,16,1]{1,2,0,3:T(8,128)(2,1)S(1)} %reshape.218, s32[6,4,1024]{2,0,1:T(8,128)S(1)} %copy.76), kind=kOutput, calls=%fused_computation.29.clone.1 | convolution fusion | flops 207618048 | bytes 393220 | tf_op jit(solution)/shard_map/while/body/eval_jaxpr/qfnb,qnk->bfk/dot_general | solution.py:97
  351.7 8.6 %fusion.33 = f32[24,256,4,16]{1,3,2,0:T(8,128)S(1)} fusion(f32[24,256,4,16]{1,3,2,0:T(8,128)S(1)} %get-tuple-element.361, s32[]{:T(128)S(6)} %copy.91, bf16[6,1024,16,1]{1,2,0,3:T(8,128)(2,1)S(1)} %reshape.218, s32[6,4,1024]{2,0,1:T(8,128)S(1)} %copy.76), kind=kOutput, calls=%fused_computation.29.clone.1 | convolution fusion | flops 207618048 | bytes 393220 | tf_op jit(solution)/shard_map/while/body/eval_jaxpr/qfnb,qnk->bfk/dot_general | solution.py:97
  364.3 8.6 %fusion.33 = f32[24,256,4,16]{1,3,2,0:T(8,128)S(1)} fusion(f32[24,256,4,16]{1,3,2,0:T(8,128)S(1)} %get-tuple-element.361, s32[]{:T(128)S(6)} %copy.91, bf16[6,1024,16,1]{1,2,0,3:T(8,128)(2,1)S(1)} %reshape.218, s32[6,4,1024]{2,0,1:T(8,128)S(1)} %copy.76), kind=kOutput, calls=%fused_computation.29.clone.1 | convolution fusion | flops 207618048 | bytes 393220 | tf_op jit(solution)/shard_map/while/body/eval_jaxpr/qfnb,qnk->bfk/dot_general | solution.py:97
  376.9 8.6 %fusion.33 = f32[24,256,4,16]{1,3,2,0:T(8,128)S(1)} fusion(f32[24,256,4,16]{1,3,2,0:T(8,128)S(1)} %get-tuple-element.361, s32[]{:T(128)S(6)} %copy.91, bf16[6,1024,16,1]{1,2,0,3:T(8,128)(2,1)S(1)} %reshape.218, s32[6,4,1024]{2,0,1:T(8,128)S(1)} %copy.76), kind=kOutput, calls=%fused_computation.29.clone.1 | convolution fusion | flops 207618048 | bytes 393220 | tf_op jit(solution)/shard_map/while/body/eval_jaxpr/qfnb,qnk->bfk/dot_general | solution.py:97
  389.4 8.6 %fusion.33 = f32[24,256,4,16]{1,3,2,0:T(8,128)S(1)} fusion(f32[24,256,4,16]{1,3,2,0:T(8,128)S(1)} %get-tuple-element.361, s32[]{:T(128)S(6)} %copy.91, bf16[6,1024,16,1]{1,2,0,3:T(8,128)(2,1)S(1)} %reshape.218, s32[6,4,1024]{2,0,1:T(8,128)S(1)} %copy.76), kind=kOutput, calls=%fused_computation.29.clone.1 | convolution fusion | flops 207618048 | bytes 393220 | tf_op jit(solution)/shard_map/while/body/eval_jaxpr/qfnb,qnk->bfk/dot_general | solution.py:97
  399.0 1.3 copy.52
  400.6 1.2 copy.54
  401.7 150.2 %all-reduce.2.cloned.1.call-done = f32[256,8,192]{0,1,2:T(8,128)} async-done(((f32[256,8,192]{0,1,2:T(8,128)}), f32[256,8,192]{0,1,2:T(8,128)}) %all-reduce.2.cloned.1.call-update) | async-done | bytes 1572880 | tf_op jit(solution)/shard_map/psum | solution.py:143
  551.9 1.8 reduce_sum.67
  554.6 1.9 reshape.215
  556.5 3.5 copy.56
  560.0 18.0 %reduce-window.16 = f32[2,8,96,2,128]{4,2,3,1,0:T(8,128)S(1)} reduce-window(f32[2,8,96,2,128]{4,2,3,1,0:T(8,128)} %copy.56, f32[]{:T(128)} %constant.15.clone.1), window={size=1x1x1x1x128 pad=0_0x0_0x0_0x0_0x127_0}, to_apply=%region_13.14 | reduce-window | flops 49938432 | bytes 3145732 | tf_op jit(solution)/shard_map/reduce-window.2
  578.0 1.6 slice.37
  579.6 2.0 copy.57
  583.1 1.2 copy.64
  584.2 17.5 %pmax.7 = f32[8]{0:T(128)} all-reduce(f32[8]{0:T(128)S(1)} %subtract_reduce_fusion), channel_id=1, replica_groups=mesh['row'=32,'feat'=8] {'feat'}, use_global_device_ids=true, to_apply=%region_17.18 | all-reduce | flops 8 | bytes 64 | tf_op jit(solution)/shard_map/pmax | solution.py:148
  (238 shorter events, 75.5 us)
Async XLA Ops:
  7.2 544.8 %all-reduce.2.cloned.1.call-start = ((), (), s32[]{:S(2)}) async-start(), calls=%async_computation | async-start | bytes 3145728 | tf_op jit(solution)/shard_map/psum | solution.py:143
  22.8 72.8 %copy-start.3 = (s32[6,1024]{1,0:T(8,128)S(1)}, s32[6,1024]{1,0:T(8,128)}, u32[]{:S(2)}) copy-start(s32[6,1024]{1,0:T(8,128)} %param.15) | copy-start | bytes 73732
  399.0 1.3 copy-start.4
  399.0 1.5 copy-start.2
  551.9 2.1 copy-start
  579.6 2.6 copy-start.1
Sparse Core Ops, SparseCore 0:
  400.5 151.4 all-reduce.1
where the time goes:
time: 613 us; the launch traced here: 609 us
  matrix products  207 us (34%)
  waiting for transfers between devices  150 us (24%)
  other arithmetic  77.6 us (13%)
  local copies, waits for them, and re-layouts  76.8 us (13%)
  loops' own time  64.7 us (11%)
  blocking collectives  17.5 us (3%)
  between operations  14.3 us (2%)
    dot_general x24, matrix products, one_block(): jnp.einsum('qfnb,qnk->bfk', one_hot, weights, preferred_element_type=jnp....  207 us
    psum x1, waiting for transfers between devices, shards(): all_bins = lax.psum(bin_histogram(bin_codes, weights, bin_total), 'row')  150 us
    another operation x1, loops' own time, bin_histogram(): lax.map(one_block, jnp.arange(feat_dev // feat_block, dtype=jnp.int32) *...  47.8 us
    reduce_sum x8, other arithmetic, pair_block(): jnp.sum(jnp.where(live_pair, pair_prob * (1.0 - pair_prob) * pair_weight,...  35.9 us
    another operation x8, other arithmetic  28 us
    dynamic_slice x48, local copies, waits for them, and re-layouts, one_block(): code_block = lax.dynamic_slice_in_dim(bin_codes, first_feat, feat_block, 1)  26.2 us
    pmax x1, blocking collectives, shards(): best_gain = lax.pmax(jnp.max(gains, axis=(0, 2)), 'feat')  17.5 us
    another operation x1, loops' own time, shards(): lax.map(block_terms, jnp.arange(feat_count, dtype=jnp.int32) * row_span)  16.9 us
  transfers between devices with their start and end apart: 1, of which 1 were waited for; matrix products, arithmetic and copies ran while one was open for 0% of the time, Pallas kernels for 0%

commit v1 on v0

v1 whole, which is shorter than its diff:
```python
import jax
import jax.numpy as jnp
from jax import lax
from jax.experimental import pallas as pl
from jax.experimental.pallas import tpu as pltpu
from jax.sharding import PartitionSpec as P

levels = 5
reg_lambda = 1.0
BI = 64
BJ = 256


def node_column(smaller_ref, parents):
    which = lax.broadcasted_iota(jnp.int32, (parents, 1), 0)
    column = jnp.zeros((parents, 1), jnp.int32)
    for p in range(parents):
        column = jnp.where(which == p, smaller_ref[p], column)
    return column


def lambda_kernel(
    counts_ref, smaller_ref, scores_ref, labels_ref, child_ref, weight_ref,
    exp_row, gain_row, disc_row, exp_col, gain_col, disc_col, row_grad, row_hess, col_grad, col_hess,
):
    query_dev, slots = scores_ref.shape
    parents = smaller_ref.shape[0]
    position = lax.broadcasted_iota(jnp.int32, (1, slots), 1)
    discount = 1.0 / jnp.log2(position.astype(jnp.float32) + 2.0)
    exp_row[...] = jnp.zeros_like(exp_row)
    gain_row[...] = jnp.zeros_like(gain_row)
    exp_row[0:query_dev, :] = jnp.exp(scores_ref[...])
    gain_row[0:query_dev, :] = jnp.exp2(labels_ref[...].astype(jnp.float32)) - 1.0
    exp_col[...] = exp_row[...].T
    gain_col[...] = gain_row[...].T
    disc_col[...] = jnp.broadcast_to(discount, (8, slots)).T
    row_grad[...] = jnp.zeros_like(row_grad)
    row_hess[...] = jnp.zeros_like(row_hess)
    col_grad[...] = jnp.zeros_like(col_grad)
    col_hess[...] = jnp.zeros_like(col_hess)
    for q in range(query_dev):
        disc_row[q : q + 1, :] = jnp.where(position < counts_ref[q], discount, 4.0)

    for q in range(query_dev):
        count = counts_ref[q]

        def row_block(ib, carry, q=q, count=count):
            first = pl.multiple_of(ib * BI, BI)
            e_i = jnp.broadcast_to(exp_col[pl.ds(first, BI), q : q + 1], (BI, BJ))
            g_i = jnp.broadcast_to(gain_col[pl.ds(first, BI), q : q + 1], (BI, BJ))
            d_i = jnp.broadcast_to(disc_col[pl.ds(first, BI), 0:1], (BI, BJ))

            def pair_tile(jb, sums):
                grad_sum, hess_sum = sums
                at = pl.multiple_of(jb * BJ, BJ)
                e_j = exp_row[q : q + 1, pl.ds(at, BJ)]
                g_j = gain_row[q : q + 1, pl.ds(at, BJ)]
                d_j = disc_row[q : q + 1, pl.ds(at, BJ)]
                inverse = 1.0 / (e_i + e_j)
                gain_gap = g_i - g_j
                disc_gap = jnp.maximum(d_i - d_j, 0.0)
                higher = gain_gap > 0.0
                part = gain_gap * disc_gap * inverse
                grad = part * jnp.where(higher, e_j, e_i)
                hess = jnp.abs(grad) * (inverse * jnp.where(higher, e_i, e_j))
                col_grad[q, :, pl.ds(at, BJ)] += jnp.sum(grad.reshape(BI // 8, 8, BJ), axis=0)
                col_hess[q, :, pl.ds(at, BJ)] += jnp.sum(hess.reshape(BI // 8, 8, BJ), axis=0)
                for k in range(0, BJ, 128):
                    grad_sum = grad_sum + grad[:, k : k + 128]
                    hess_sum = hess_sum + hess[:, k : k + 128]
                return grad_sum, hess_sum

            zero = jnp.zeros((BI, 128), jnp.float32)
            grad_sum, hess_sum = lax.fori_loop(
                (ib * BI) // BJ, (count + BJ - 1) // BJ, pair_tile, (zero, zero)
            )
            row_grad[pl.ds(first, BI), q : q + 1] = jnp.sum(grad_sum, axis=1, keepdims=True)
            row_hess[pl.ds(first, BI), q : q + 1] = jnp.sum(hess_sum, axis=1, keepdims=True)
            return carry

        lax.fori_loop(0, (count + BI - 1) // BI, row_block, 0)

    row_grad_t = row_grad[...].T
    row_hess_t = row_hess[...].T
    nodes = 2 * lax.broadcasted_iota(jnp.int32, (parents, 1), 0) + node_column(smaller_ref, parents)
    for q in range(query_dev):
        grade = labels_ref[q : q + 1, :]
        usable = position < counts_ref[q]
        ideal = jnp.zeros((1, slots), jnp.float32)
        ahead = jnp.zeros((1, 1), jnp.int32)
        for c in range(levels - 1, 0, -1):
            here = jnp.sum(((grade == c) & usable).astype(jnp.int32), axis=1, keepdims=True)
            span = (position >= ahead) & (position < ahead + here)
            ideal = ideal + jnp.where(span, float(2**c - 1), 0.0)
            ahead = ahead + here
        inv_ideal = 1.0 / jnp.maximum(jnp.sum(ideal * discount, axis=1, keepdims=True), 1.0)
        grad = (jnp.sum(col_grad[q], axis=0, keepdims=True) - row_grad_t[q : q + 1, :]) * inv_ideal
        hess = (jnp.sum(col_hess[q], axis=0, keepdims=True) + row_hess_t[q : q + 1, :]) * inv_ideal
        member = child_ref[q : q + 1, :] == nodes
        both = jnp.concatenate((jnp.where(member, grad, 0.0), jnp.where(member, hess, 0.0)), axis=0)
        weight_ref[:, q * slots : (q + 1) * slots] = both.astype(jnp.bfloat16)


def lambda_weights(scores, labels, counts, row_child, smaller):
    query_dev, slots = scores.shape
    parents = smaller.shape[0]
    vmem = pl.BlockSpec(memory_space=pltpu.VMEM)
    smem = pl.BlockSpec(memory_space=pltpu.SMEM)
    row = pltpu.VMEM((8, slots), jnp.float32)
    col = pltpu.VMEM((slots, 8), jnp.float32)
    acc = pltpu.VMEM((query_dev, 8, slots), jnp.float32)
    return pl.pallas_call(
        lambda_kernel,
        out_shape=jax.ShapeDtypeStruct((2 * parents, query_dev * slots), jnp.bfloat16),
        in_specs=[smem, smem, vmem, vmem, vmem],
        out_specs=vmem,
        scratch_shapes=[row, row, row, col, col, col, col, col, acc, acc],
        name="lambda_weights",
    )(counts, smaller, scores, labels, row_child)


def histogram_kernel(codes_ref, weight_ref, hist_ref):
    query_dev, feats, slots = codes_ref.shape
    one = jnp.ones((), jnp.bfloat16)
    zero = jnp.zeros((), jnp.bfloat16)
    low_mark = lax.broadcasted_iota(jnp.int32, (64, 1), 0).astype(jnp.float32).astype(jnp.bfloat16)
    for group in range(feats // 4):
        total = jnp.zeros((256, 256), jnp.float32)
        for q in range(query_dev):
            weight = weight_ref[:, q * slots : (q + 1) * slots]
            lhs = []
            rhs = []
            for f in range(4 * group, 4 * group + 4):
                code = codes_ref[q, f : f + 1, :]
                high = jnp.broadcast_to((code >> 6).astype(jnp.float32), (16, slots)).astype(jnp.bfloat16)
                low = jnp.broadcast_to((code & 63).astype(jnp.float32), (64, slots)).astype(jnp.bfloat16)
                for h in range(4):
                    lhs.append(jnp.where(high == jnp.asarray(h, jnp.bfloat16), weight, zero))
                rhs.append(jnp.where(low == low_mark, one, zero))
            total += lax.dot_general(
                jnp.concatenate(lhs, axis=0), jnp.concatenate(rhs, axis=0),
                (((1,), (1,)), ((), ())), preferred_element_type=jnp.float32,
            )
        for k in range(4):
            pieces = [total[k * 64 + h * 16 : k * 64 + h * 16 + 16, k * 64 : k * 64 + 64] for h in range(4)]
            hist_ref[4 * group + k] = jnp.concatenate(pieces, axis=1).astype(jnp.bfloat16)


def histograms(bin_codes, weight):
    query_dev, feat_dev, slots = bin_codes.shape
    return pl.pallas_call(
        histogram_kernel,
        grid=(feat_dev // 8,),
        out_shape=jax.ShapeDtypeStruct((feat_dev, 16, 256), jnp.bfloat16),
        in_specs=[
            pl.BlockSpec((query_dev, 8, slots), lambda i: (0, i, 0)),
            pl.BlockSpec(weight.shape, lambda i: (0, 0)),
        ],
        out_specs=pl.BlockSpec((8, 16, 256), lambda i: (i, 0, 0)),
        name="histograms",
    )(bin_codes, weight)


def gain_kernel(parts_ref, send_ref):
    sources, rows, bins = parts_ref.shape
    built = jnp.sum(parts_ref[...].astype(jnp.float32), axis=0)
    below = lax.broadcasted_iota(jnp.int32, (bins, bins), 0)
    upto = lax.broadcasted_iota(jnp.int32, (bins, bins), 1)
    left = jnp.dot(
        built, (below <= upto).astype(jnp.float32),
        precision=lax.Precision.HIGHEST, preferred_element_type=jnp.float32,
    )
    threshold = lax.broadcasted_iota(jnp.int32, (8, bins), 1)
    best = jnp.full((8, 1), -jnp.inf, jnp.float32)
    for f in range(rows // 16):
        grad_left = left[f * 16 : f * 16 + 8]
        hess_left = left[f * 16 + 8 : f * 16 + 16]
        grad_total = grad_left[:, bins - 1 : bins]
        hess_total = hess_left[:, bins - 1 : bins]
        grad_right = grad_total - grad_left
        gain = (
            grad_left * grad_left / (hess_left + reg_lambda)
            + grad_right * grad_right / (hess_total - hess_left + reg_lambda)
            - grad_total * grad_total / (hess_total + reg_lambda)
        )
        gain = jnp.where(threshold < bins - 1, gain, -jnp.inf)
        best = jnp.maximum(best, jnp.max(gain, axis=1, keepdims=True))
    stacked = jnp.concatenate(
        (built, jnp.broadcast_to(best, (8, bins)), jnp.zeros((128 - rows - 8, bins), jnp.float32)), axis=0
    )
    send_ref[...] = stacked.T.reshape(send_ref.shape)


def children_kernel(smaller_ref, parts_ref, parent_ref, children_ref, best_ref):
    sources, bin_span, lanes = parts_ref.shape
    parents, width = children_ref.shape[1:]
    group = width // sources
    column = lax.broadcasted_iota(jnp.int32, (sources, width), 1)
    source = lax.broadcasted_iota(jnp.int32, (sources, width), 0)
    spread = (column // group == source).astype(jnp.float32)
    rows = group * parents // 2
    row = lax.broadcasted_iota(jnp.int32, (rows, width), 0)
    col = lax.broadcasted_iota(jnp.int32, (rows, width), 1)
    match = (row // (2 * parents) == (col % group) // 4) & ((row // parents) % 2 == col % 2)
    pick_row = lax.broadcasted_iota(jnp.int32, (width // 2, width), 0)
    pick_col = lax.broadcasted_iota(jnp.int32, (width // 2, width), 1)
    pick = (pick_row == (pick_col // 4) * 2 + pick_col % 2).astype(jnp.float32)
    side = (lax.broadcasted_iota(jnp.int32, (parents, width), 1) // 2) % 2
    chosen = side == node_column(smaller_ref, parents)
    parent = jnp.dot(
        parent_ref[...].reshape(bin_span * parents, width // 2), pick,
        precision=lax.Precision.HIGHEST, preferred_element_type=jnp.float32,
    )
    for b in range(bin_span):
        wide = lax.dot_general(
            parts_ref[:, b, :], spread, (((0,), (0,)), ((), ())),
            precision=lax.Precision.HIGHEST, preferred_element_type=jnp.float32,
        )
        kept = jnp.where(match, wide[:rows], 0.0)
        built = jnp.sum(kept.reshape(rows // parents, parents, width), axis=0)
        children_ref[b] = jnp.where(chosen, built, parent[b * parents : (b + 1) * parents] - built)
    best = jnp.max(parts_ref[:, 0, :], axis=0, keepdims=True)
    best_ref[...] = jnp.broadcast_to(best[None], best_ref.shape)


def shards(scores, labels, counts, bin_codes, row_child, smaller, parent_hist):
    feat_dev = bin_codes.shape[1]
    bin_span, parents, _ = parent_hist.shape
    row_count = lax.axis_size("row")
    feat_count = lax.axis_size("feat")
    rows = feat_dev // row_count * 2 * parents
    bins = bin_span * row_count
    weight = lambda_weights(scores, labels, counts, row_child, smaller)
    hist = histograms(bin_codes, weight)
    parts = lax.all_to_all(hist.reshape(row_count, rows, bins), "row", 0, 0, tiled=True)
    vmem = pl.BlockSpec(memory_space=pltpu.VMEM)
    smem = pl.BlockSpec(memory_space=pltpu.SMEM)
    send = pl.pallas_call(
        gain_kernel,
        out_shape=jax.ShapeDtypeStruct((row_count, bin_span, 128), jnp.float32),
        in_specs=[vmem], out_specs=vmem, name="gains",
    )(parts)
    own = lax.all_to_all(send, "row", 0, 0, tiled=True)
    children, best = pl.pallas_call(
        children_kernel,
        out_shape=(
            jax.ShapeDtypeStruct((bin_span, parents, feat_dev * 4), jnp.float32),
            jax.ShapeDtypeStruct((feat_count, 8, 128), jnp.float32),
        ),
        in_specs=[smem, vmem, vmem], out_specs=(vmem, vmem), name="children",
    )(smaller, own, parent_hist)
    best = jnp.max(lax.all_to_all(best, "feat", 0, 0, tiled=True), axis=0)
    return children, best[0, rows : rows + parents]


def solution(mesh):
    placed = (
        P("row", None), P("row", None), P("row"), P("row", "feat", None),
        P("row", None), P(), P("row", None, "feat"),
    )
    return jax.shard_map(
        shards, mesh=mesh, in_specs=placed, out_specs=(P("row", None, "feat"), P()), check_vma=False
    )
```

time: 613 us -> 123 us (0.20)
  matrix products: 207 us -> 0 us
  waiting for transfers between devices: 150 us -> 0 us
  other arithmetic: 77.6 us -> 0.01 us
  local copies, waits for them, and re-layouts: 76.8 us -> 0.58 us
  loops' own time: 64.7 us -> 0 us
  Pallas kernels: 0 us -> 52.5 us
  blocking collectives: 17.5 us -> 68.2 us
  between operations: 14.3 us -> 0.63 us
    dot_general x24 -> x0, matrix products: 207 us -> none  [one_block(): jnp.einsum('qfnb,qnk->bfk', one_hot, weights, preferred_element_type=jnp....]
    psum x1 -> x0, waiting for transfers between devices: 150 us -> none  [shards(): all_bins = lax.psum(bin_histogram(bin_codes, weights, bin_total), 'row')]
    all_to_all x0 -> x3, blocking collectives: none -> 68.2 us  [the longest x1 38.9 us: shards(): lax.all_to_all(hist.reshape(row_count, rows, bins), 'row', 0, 0, tiled=True)]
    another operation x2 -> x0, loops' own time: 64.7 us -> none  [the longest x1 47.8 us: bin_histogram(): lax.map(one_block, jnp.arange(feat_dev // feat_block, dtype=jnp.int32) *...]
    dynamic_slice x114 -> x0, local copies, waits for them, and re-layouts: 59.6 us -> none  [the longest x48 26.2 us: one_block(): code_block = lax.dynamic_slice_in_dim(bin_codes, first_feat, feat_block, 1)]
    pallas_call x0 -> x4, Pallas kernels: none -> 52.5 us  [the longest x1 24.7 us: histograms(): pl.pallas_call(histogram_kernel, grid=(feat_dev // 8,), out_shape=jax.Sha...]
    reduce_sum x12 -> x0, other arithmetic: 40.5 us -> none  [the longest x8 35.9 us: pair_block(): jnp.sum(jnp.where(live_pair, pair_prob * (1.0 - pair_prob) * pair_weight,...]
    another operation x9 -> x0, other arithmetic: 28 us -> none
  transfers between devices with their start and end apart: 1 -> 0, of which waited for: 1 -> 0; matrix products, arithmetic and copies ran while one was open for 0% -> 0% of each run, Pallas kernels for 0% -> 0%
where the time goes in v1:
time: 123 us; the launch traced here: 122 us
  blocking collectives  68.2 us (55%)
  Pallas kernels  52.5 us (43%)
    all_to_all x1, blocking collectives, shards(): lax.all_to_all(hist.reshape(row_count, rows, bins), 'row', 0, 0, tiled=True)  38.9 us
    pallas_call x1, Pallas kernels, histograms(): pl.pallas_call(histogram_kernel, grid=(feat_dev // 8,), out_shape=jax.Sha...  24.7 us
    pallas_call x1, Pallas kernels, lambda_weights(): pl.pallas_call(lambda_kernel, out_shape=jax.ShapeDtypeStruct((2 * parents...  22.4 us
    all_to_all x1, blocking collectives, shards(): own = lax.all_to_all(send, 'row', 0, 0, tiled=True)  17.5 us
    all_to_all x1, blocking collectives, shards(): best = jnp.max(lax.all_to_all(best, 'feat', 0, 0, tiled=True), axis=0)  11.9 us
    pallas_call x1, Pallas kernels, shards(): pl.pallas_call(children_kernel, out_shape=(jax.ShapeDtypeStruct((bin_span...  3.14 us

profile of v1, /device:TPU:1, one launch (start us, length us, event | category | flops | bytes accessed | tf_op | source)
XLA Modules:
  0.0 122.0 jit_solution(7946536487269173102)
XLA Ops:
  0.6 22.4 %lambda_weights.1.weight_ref = bf16[16,6144]{1,0:T(8,128)(2,1)} custom-call(s32[6]{0:T(128)} %counts_ref.1, s32[8]{0:T(128)} %smaller_ref.3, f32[6,1024]{1,0:T(8,128)} %scores_ref.1, s32[6,1024]{1,0:T(8,128)} %labels_ref.1, s32[6,1024]{1,0:T(8,128)} %child_ref.1), custom_call_target="tpu_custom_call" | custom-call | tf_op jit(solution)/shard_map/lambda_weights/pallas_call | solution.py:112
  23.0 24.7 %histograms.1 = bf16[96,16,256]{2,1,0:T(8,128)(2,1)} custom-call(s32[6,96,1024]{2,1,0:T(8,128)} %codes_ref.1, bf16[16,6144]{1,0:T(8,128)(2,1)} %lambda_weights.1.weight_ref), custom_call_target="tpu_custom_call" | custom-call | tf_op jit(solution)/shard_map/histograms/pallas_call | solution.py:151
  47.7 38.9 %all_to_all.15.parts_ref = bf16[32,48,256]{2,1,0:T(8,128)(2,1)} all-to-all(bf16[32,48,256]{2,1,0:T(8,128)(2,1)} %bitcast.3), channel_id=1, replica_groups=mesh['row'=32,'feat'=8] {'row'}, dimensions={0} | all-to-all | bytes 1572864 | tf_op jit(solution)/shard_map/all_to_all | solution.py:235
  86.6 2.4 %gains.1 = f32[32,8,128]{2,1,0:T(8,128)} custom-call(bf16[32,48,256]{2,1,0:T(8,128)(2,1)} %all_to_all.15.parts_ref), custom_call_target="tpu_custom_call" | custom-call | tf_op jit(solution)/shard_map/gains/pallas_call | solution.py:238
  88.9 17.5 %all_to_all.16.parts_ref = f32[32,8,128]{2,1,0:T(8,128)} all-to-all(f32[32,8,128]{2,1,0:T(8,128)} %gains.1), channel_id=1, replica_groups=mesh['row'=32,'feat'=8] {'row'}, dimensions={0} | all-to-all | bytes 262144 | tf_op jit(solution)/shard_map/all_to_all | solution.py:243
  106.4 3.1 %children.1 = (f32[8,8,384]{2,1,0:T(8,128)}, f32[8,8,128]{2,1,0:T(8,128)}) custom-call(s32[8]{0:T(128)} %smaller_ref.3, f32[32,8,128]{2,1,0:T(8,128)} %all_to_all.16.parts_ref, f32[8,8,192]{2,1,0:T(8,128)} %parent_ref.1), custom_call_target="tpu_custom_call" | custom-call | tf_op jit(solution)/shard_map/children/pallas_call | solution.py:244
  109.5 11.9 %all_to_all.17 = f32[8,8,128]{2,1,0:T(8,128)S(1)} all-to-all(f32[8,8,128]{2,1,0:T(8,128)} %get-tuple-element.5), channel_id=1, replica_groups=mesh['row'=32,'feat'=8] {'feat'}, dimensions={0} | all-to-all | bytes 65536 | tf_op jit(solution)/shard_map/all_to_all | solution.py:252
  121.4 0.6 slice_bitcast_fusion
  (1 shorter events, 0.0 us)

commit v2 on v1

v2 whole, which is shorter than its diff:
```python
import jax
import jax.numpy as jnp
from jax import lax
from jax.experimental import pallas as pl
from jax.experimental.pallas import tpu as pltpu
from jax.sharding import PartitionSpec as P

levels = 5
reg_lambda = 1.0
SHARE = 128
EARLY = 2


def node_column(smaller_ref, parents):
    which = lax.broadcasted_iota(jnp.int32, (parents, 1), 0)
    column = jnp.zeros((parents, 1), jnp.int32)
    for p in range(parents):
        column = jnp.where(which == p, smaller_ref[p], column)
    return column


def lambda_kernel(
    counts_ref, scores_ref, labels_ref, lam_ref,
    exp_row, gain_row, disc_row, exp_col, gain_col, disc_col, lam_rows,
):
    query_dev, slots = scores_ref.shape
    own = pl.multiple_of(lax.axis_index("feat") * SHARE, SHARE)
    position = lax.broadcasted_iota(jnp.int32, (1, slots), 1)
    discount = 1.0 / jnp.log2(position.astype(jnp.float32) + 2.0)
    disc_row[...] = jnp.broadcast_to(discount, (8, slots))
    exp_row[...] = jnp.zeros_like(exp_row)
    gain_row[...] = jnp.zeros_like(gain_row)
    lam_rows[...] = jnp.zeros_like(lam_rows)
    score_exp = jnp.exp(scores_ref[...])
    rel_gain = jnp.exp2(labels_ref[...].astype(jnp.float32)) - 1.0
    for q in range(query_dev):
        usable = position < counts_ref[q]
        exp_row[q : q + 1, :] = jnp.where(usable, score_exp[q : q + 1], 0.0)
        gain_row[q : q + 1, :] = jnp.where(usable, rel_gain[q : q + 1], -1.0)
    exp_col[...] = exp_row[...].T
    gain_col[...] = gain_row[...].T
    disc_col[...] = disc_row[...].T

    for q in range(query_dev):
        count = counts_ref[q]
        e_i = exp_row[q : q + 1, pl.ds(own, SHARE)]
        g_i = gain_row[q : q + 1, pl.ds(own, SHARE)]
        d_i = disc_row[0:1, pl.ds(own, SHARE)]

        def partners(jb, sums, q=q, e_i=e_i, g_i=g_i, d_i=d_i):
            grad_sum, hess_sum = sums
            at = pl.multiple_of(jb * 128, 128)
            e_j = exp_col[pl.ds(at, 128), q : q + 1]
            g_j = gain_col[pl.ds(at, 128), q : q + 1]
            d_j = disc_col[pl.ds(at, 128), 0:1]
            inverse = 1.0 / (e_i + e_j)
            gain_gap = g_i - g_j
            higher = gain_gap > 0.0
            part = gain_gap * (jnp.abs(d_i - d_j) * inverse)
            grad = part * jnp.where(higher, e_j, e_i)
            hess = jnp.abs(grad) * (inverse * jnp.where(higher, e_i, e_j))
            grad_sum = grad_sum + jnp.sum(grad.reshape(16, 8, SHARE), axis=0)
            hess_sum = hess_sum + jnp.sum(hess.reshape(16, 8, SHARE), axis=0)
            return grad_sum, hess_sum

        zero = jnp.zeros((8, SHARE), jnp.float32)
        last = jnp.where(own < count, (count + 127) // 128, 0)
        grad_sum, hess_sum = lax.fori_loop(0, last, partners, (zero, zero))

        grade = labels_ref[q : q + 1, :]
        usable = position < count
        ideal = jnp.zeros((1, slots), jnp.float32)
        ahead = jnp.zeros((1, 1), jnp.int32)
        for c in range(levels - 1, 0, -1):
            here = jnp.sum(((grade == c) & usable).astype(jnp.int32), axis=1, keepdims=True)
            span = (position >= ahead) & (position < ahead + here)
            ideal = ideal + jnp.where(span, float(2**c - 1), 0.0)
            ahead = ahead + here
        inv_ideal = 1.0 / jnp.maximum(jnp.sum(ideal * discount, axis=1, keepdims=True), 1.0)
        mine = own + lax.broadcasted_iota(jnp.int32, (1, SHARE), 1) < count
        grad = -jnp.sum(grad_sum, axis=0, keepdims=True) * inv_ideal
        hess = jnp.sum(hess_sum, axis=0, keepdims=True) * inv_ideal
        lam_rows[q : q + 1, :] = jnp.where(mine, grad, 0.0)
        lam_rows[8 + q : 9 + q, :] = jnp.where(mine, hess, 0.0)

    lam_ref[...] = jnp.broadcast_to(lam_rows[...].astype(jnp.bfloat16)[None], lam_ref.shape)


def lambdas(scores, labels, counts):
    query_dev, slots = scores.shape
    vmem = pl.BlockSpec(memory_space=pltpu.VMEM)
    smem = pl.BlockSpec(memory_space=pltpu.SMEM)
    row = pltpu.VMEM((8, slots), jnp.float32)
    col = pltpu.VMEM((slots, 8), jnp.float32)
    return pl.pallas_call(
        lambda_kernel,
        out_shape=jax.ShapeDtypeStruct((slots // SHARE, 16, SHARE), jnp.bfloat16),
        in_specs=[smem, vmem, vmem],
        out_specs=vmem,
        scratch_shapes=[row, row, row, col, col, col, pltpu.VMEM((16, SHARE), jnp.float32)],
        name="lambdas",
    )(counts, scores, labels)


def weight_kernel(smaller_ref, lam_ref, child_ref, weight_ref):
    query_dev, slots = child_ref.shape
    parents = smaller_ref.shape[0]
    nodes = 2 * lax.broadcasted_iota(jnp.int32, (parents, 1), 0) + node_column(smaller_ref, parents)
    lam = jnp.concatenate([lam_ref[k].astype(jnp.float32) for k in range(lam_ref.shape[0])], axis=1)
    for q in range(query_dev):
        member = child_ref[q : q + 1, :] == nodes
        grad = jnp.where(member, lam[q : q + 1], 0.0)
        hess = jnp.where(member, lam[8 + q : 9 + q], 0.0)
        weight_ref[:, q * slots : (q + 1) * slots] = jnp.concatenate((grad, hess), axis=0).astype(jnp.bfloat16)


def histogram_kernel(codes_ref, weight_ref, after_ref, hist_ref):
    del after_ref
    query_dev, feats, slots = codes_ref.shape
    one = jnp.ones((), jnp.bfloat16)
    zero = jnp.zeros((), jnp.bfloat16)
    low_mark = lax.broadcasted_iota(jnp.int32, (64, 1), 0).astype(jnp.float32).astype(jnp.bfloat16)
    for group in range(feats // 4):
        total = jnp.zeros((256, 256), jnp.float32)
        for q in range(query_dev):
            weight = weight_ref[:, q * slots : (q + 1) * slots]
            lhs = []
            rhs = []
            for f in range(4 * group, 4 * group + 4):
                code = codes_ref[q, f : f + 1, :]
                high = jnp.broadcast_to((code >> 6).astype(jnp.float32), (16, slots)).astype(jnp.bfloat16)
                low = jnp.broadcast_to((code & 63).astype(jnp.float32), (64, slots)).astype(jnp.bfloat16)
                for h in range(4):
                    lhs.append(jnp.where(high == jnp.asarray(h, jnp.bfloat16), weight, zero))
                rhs.append(jnp.where(low == low_mark, one, zero))
            total += lax.dot_general(
                jnp.concatenate(lhs, axis=0), jnp.concatenate(rhs, axis=0),
                (((1,), (1,)), ((), ())), preferred_element_type=jnp.float32,
            )
        for k in range(4):
            pieces = [total[k * 64 + h * 16 : k * 64 + h * 16 + 16, k * 64 : k * 64 + 64] for h in range(4)]
            hist_ref[4 * group + k] = jnp.concatenate(pieces, axis=1).astype(jnp.bfloat16)


def histograms(bin_codes, weight, after, first, count):
    query_dev, feat_dev, slots = bin_codes.shape
    return pl.pallas_call(
        histogram_kernel,
        grid=(count // 8,),
        out_shape=jax.ShapeDtypeStruct((count, 16, 256), jnp.bfloat16),
        in_specs=[
            pl.BlockSpec((query_dev, 8, slots), lambda i: (0, i + first // 8, 0)),
            pl.BlockSpec(weight.shape, lambda i: (0, 0)),
            pl.BlockSpec(memory_space=pl.ANY),
        ],
        out_specs=pl.BlockSpec((8, 16, 256), lambda i: (i, 0, 0)),
        name="histograms",
    )(bin_codes, weight, after)


def gain_kernel(early_ref, late_ref, send_ref):
    rows = early_ref.shape[1] + late_ref.shape[1]
    bins = early_ref.shape[2]
    built = jnp.concatenate(
        (
            jnp.sum(early_ref[...].astype(jnp.float32), axis=0),
            jnp.sum(late_ref[...].astype(jnp.float32), axis=0),
        ),
        axis=0,
    )
    below = lax.broadcasted_iota(jnp.int32, (bins, bins), 0)
    upto = lax.broadcasted_iota(jnp.int32, (bins, bins), 1)
    left = jnp.dot(
        built, (below <= upto).astype(jnp.float32),
        precision=lax.Precision.HIGHEST, preferred_element_type=jnp.float32,
    )
    threshold = lax.broadcasted_iota(jnp.int32, (8, bins), 1)
    best = jnp.full((8, 1), -jnp.inf, jnp.float32)
    for f in range(rows // 16):
        grad_left = left[f * 16 : f * 16 + 8]
        hess_left = left[f * 16 + 8 : f * 16 + 16]
        grad_total = grad_left[:, bins - 1 : bins]
        hess_total = hess_left[:, bins - 1 : bins]
        grad_right = grad_total - grad_left
        gain = (
            grad_left * grad_left / (hess_left + reg_lambda)
            + grad_right * grad_right / (hess_total - hess_left + reg_lambda)
            - grad_total * grad_total / (hess_total + reg_lambda)
        )
        gain = jnp.where(threshold < bins - 1, gain, -jnp.inf)
        best = jnp.maximum(best, jnp.max(gain, axis=1, keepdims=True))
    stacked = jnp.concatenate(
        (built, jnp.broadcast_to(best, (8, bins)), jnp.zeros((128 - rows - 8, bins), jnp.float32)), axis=0
    )
    send_ref[...] = stacked.T.reshape(send_ref.shape)


def children_kernel(smaller_ref, parts_ref, parent_ref, children_ref):
    sources, bin_span, lanes = parts_ref.shape
    parents, width = children_ref.shape[1:]
    group = width // sources
    early = EARLY * sources

    def place(column):
        feat = column // 4
        is_early = feat < early
        owner = jnp.where(is_early, feat // EARLY, (feat - early) % sources)
        local = jnp.where(is_early, feat % EARLY, EARLY + (feat - early) // sources)
        return owner, local

    column = lax.broadcasted_iota(jnp.int32, (sources, width), 1)
    source = lax.broadcasted_iota(jnp.int32, (sources, width), 0)
    spread = (place(column)[0] == source).astype(jnp.float32)
    rows = group * parents // 2
    row = lax.broadcasted_iota(jnp.int32, (rows, width), 0)
    col = lax.broadcasted_iota(jnp.int32, (rows, width), 1)
    match = (row // (2 * parents) == place(col)[1]) & ((row // parents) % 2 == col % 2)
    pick_row = lax.broadcasted_iota(jnp.int32, (width // 2, width), 0)
    pick_col = lax.broadcasted_iota(jnp.int32, (width // 2, width), 1)
    pick = (pick_row == (pick_col // 4) * 2 + pick_col % 2).astype(jnp.float32)
    side = (lax.broadcasted_iota(jnp.int32, (parents, width), 1) // 2) % 2
    chosen = side == node_column(smaller_ref, parents)
    parent = jnp.dot(
        parent_ref[...].reshape(bin_span * parents, width // 2), pick,
        precision=lax.Precision.HIGHEST, preferred_element_type=jnp.float32,
    )
    for b in range(bin_span):
        wide = lax.dot_general(
            parts_ref[:, b, :], spread, (((0,), (0,)), ((), ())),
            precision=lax.Precision.HIGHEST, preferred_element_type=jnp.float32,
        )
        kept = jnp.where(match, wide[:rows], 0.0)
        built = jnp.sum(kept.reshape(rows // parents, parents, width), axis=0)
        children_ref[b] = jnp.where(chosen, built, parent[b * parents : (b + 1) * parents] - built)


def shards(scores, labels, counts, bin_codes, row_child, smaller, parent_hist):
    feat_dev = bin_codes.shape[1]
    bin_span, parents, _ = parent_hist.shape
    row_count = lax.axis_size("row")
    feat_count = lax.axis_size("feat")
    rows = feat_dev // row_count * 2 * parents
    bins = bin_span * row_count
    vmem = pl.BlockSpec(memory_space=pltpu.VMEM)
    smem = pl.BlockSpec(memory_space=pltpu.SMEM)
    lam = lax.all_to_all(lambdas(scores, labels, counts), "feat", 0, 0, tiled=True)
    weight = pl.pallas_call(
        weight_kernel,
        out_shape=jax.ShapeDtypeStruct((2 * parents, row_child.size), jnp.bfloat16),
        in_specs=[smem, vmem, vmem], out_specs=vmem, name="weights",
    )(smaller, lam, row_child)
    received = []
    first, hist = 0, weight
    for count in (EARLY * row_count, feat_dev - EARLY * row_count):
        hist = histograms(bin_codes, weight, hist, first, count)
        parts = hist.reshape(row_count, count // row_count * 2 * parents, bins)
        received.append(lax.all_to_all(parts, "row", 0, 0, tiled=True))
        first += count
    send = pl.pallas_call(
        gain_kernel,
        out_shape=jax.ShapeDtypeStruct((row_count, bin_span, 128), jnp.float32),
        in_specs=[vmem, vmem], out_specs=vmem, name="gains",
    )(*received)
    own = lax.all_to_all(send, "row", 0, 0, tiled=True)
    best = jnp.broadcast_to(jnp.max(own, axis=0)[None], (feat_count, bin_span, 128))
    best = jnp.max(lax.all_to_all(best, "feat", 0, 0, tiled=True), axis=0)
    children = pl.pallas_call(
        children_kernel,
        out_shape=jax.ShapeDtypeStruct((bin_span, parents, feat_dev * 4), jnp.float32),
        in_specs=[smem, vmem, vmem], out_specs=vmem, name="children",
    )(smaller, own, parent_hist)
    return children, best[0, rows : rows + parents]


def solution(mesh):
    placed = (
        P("row", None), P("row", None), P("row"), P("row", "feat", None),
        P("row", None), P(), P("row", None, "feat"),
    )
    return jax.shard_map(
        shards, mesh=mesh, in_specs=placed, out_specs=(P("row", None, "feat"), P()), check_vma=False
    )
```

time: 123 us -> 120 us (0.976)
  Pallas kernels: 52.5 us -> 41.7 us
  starting transfers between devices: 0 us -> 6.43 us
  waiting for transfers between devices: 0 us -> 1.6 us
    pallas_call x3 -> x5, Pallas kernels: 50.2 us -> 39.3 us  [the longest x2 26.4 us: histograms(): pl.pallas_call(histogram_kernel, grid=(count // 8,), out_shape=jax.ShapeD...]
    all_to_all x0 -> x1, starting transfers between devices: none -> 6.43 us  [shards(): best = jnp.max(lax.all_to_all(best, 'feat', 0, 0, tiled=True), axis=0)]
    all_to_all x0 -> x1, waiting for transfers between devices: none -> 1.6 us  [shards(): best = jnp.max(lax.all_to_all(best, 'feat', 0, 0, tiled=True), axis=0)]
    all_to_all x2 -> x3, blocking collectives: 50.7 us -> 50.2 us  [the longest x2 38.2 us: shards(): received.append(lax.all_to_all(parts, 'row', 0, 0, tiled=True))]
  transfers between devices with their start and end apart: 0 -> 1, of which waited for: 0 -> 1; matrix products, arithmetic and copies ran while one was open for 0% -> 0% of each run, Pallas kernels for 0% -> 3%
where the time goes in v2:
time: 120 us; the launch traced here: 119 us
  blocking collectives  67.8 us (56%)
  Pallas kernels  41.7 us (35%)
  starting transfers between devices  6.43 us (5%)
  waiting for transfers between devices  1.6 us (1%)
  local copies, waits for them, and re-layouts  1.21 us (1%)
    all_to_all x2, blocking collectives, shards(): received.append(lax.all_to_all(parts, 'row', 0, 0, tiled=True))  38.2 us
    pallas_call x2, Pallas kernels, histograms(): pl.pallas_call(histogram_kernel, grid=(count // 8,), out_shape=jax.ShapeD...  26.4 us
    all_to_all x1, blocking collectives, shards(): own = lax.all_to_all(send, 'row', 0, 0, tiled=True)  17.6 us
    all_to_all x1, blocking collectives, shards(): lax.all_to_all(lambdas(scores, labels, counts), 'feat', 0, 0, tiled=True)  12 us
    pallas_call x1, Pallas kernels, lambdas(): pl.pallas_call(lambda_kernel, out_shape=jax.ShapeDtypeStruct((slots // SH...  8.3 us
    all_to_all x1, starting transfers between devices, shards(): best = jnp.max(lax.all_to_all(best, 'feat', 0, 0, tiled=True), axis=0)  6.43 us
    pallas_call x1, Pallas kernels, shards(): pl.pallas_call(children_kernel, out_shape=jax.ShapeDtypeStruct((bin_span,...  3.14 us
  transfers between devices with their start and end apart: 1, of which 1 were waited for; matrix products, arithmetic and copies ran while one was open for 0% of the time, Pallas kernels for 3%

profile of v2, /device:TPU:1, one launch (start us, length us, event | category | flops | bytes accessed | tf_op | source)
XLA Modules:
  0.0 119.4 jit_solution(16435123153050255316)
XLA Ops:
  0.6 8.3 %lambdas.1 = bf16[8,16,128]{2,1,0:T(8,128)(2,1)} custom-call(s32[6]{0:T(128)} %counts_ref.1, f32[6,1024]{1,0:T(8,128)} %scores_ref.1, s32[6,1024]{1,0:T(8,128)} %labels_ref.1), custom_call_target="tpu_custom_call" | custom-call | tf_op jit(solution)/shard_map/lambdas/pallas_call | solution.py:95
  8.9 12.0 %all_to_all.25.lam_ref = bf16[8,16,128]{2,1,0:T(8,128)(2,1)} all-to-all(bf16[8,16,128]{2,1,0:T(8,128)(2,1)} %lambdas.1), channel_id=1, replica_groups=mesh['row'=32,'feat'=8] {'feat'}, dimensions={0} | all-to-all | bytes 65536 | tf_op jit(solution)/shard_map/all_to_all | solution.py:246
  20.9 1.5 %weights.1.weight_ref.after_ref = bf16[16,6144]{1,0:T(8,128)(2,1)} custom-call(s32[8]{0:T(128)} %smaller_ref.3, bf16[8,16,128]{2,1,0:T(8,128)(2,1)} %all_to_all.25.lam_ref, s32[6,1024]{1,0:T(8,128)} %child_ref.1), custom_call_target="tpu_custom_call" | custom-call | tf_op jit(solution)/shard_map/weights/pallas_call | solution.py:247
  22.4 17.0 %histograms.2.after_ref = bf16[64,16,256]{2,1,0:T(8,128)(2,1)} custom-call(s32[6,96,1024]{2,1,0:T(8,128)} %codes_ref.3, bf16[16,6144]{1,0:T(8,128)(2,1)} %weights.1.weight_ref.after_ref, bf16[16,6144]{1,0:T(8,128)(2,1)} %weights.1.weight_ref.after_ref), custom_call_target="tpu_custom_call" | custom-call | tf_op jit(solution)/shard_map/histograms/pallas_call | solution.py:147
  39.4 0.0 copy-start
  39.4 9.4 %histograms.3 = bf16[32,16,256]{2,1,0:T(8,128)(2,1)} custom-call(s32[6,96,1024]{2,1,0:T(8,128)} %codes_ref.3, bf16[16,6144]{1,0:T(8,128)(2,1)} %weights.1.weight_ref.after_ref, bf16[64,16,256]{2,1,0:T(8,128)(2,1)} %histograms.2.after_ref), custom_call_target="tpu_custom_call" | custom-call | tf_op jit(solution)/shard_map/histograms/pallas_call | solution.py:147
  48.8 19.1 %all_to_all.26.late_ref = bf16[32,16,256]{2,1,0:T(8,128)(2,1)} all-to-all(bf16[32,16,256]{2,1,0:T(8,128)(2,1)} %histograms.3), channel_id=1, replica_groups=mesh['row'=32,'feat'=8] {'row'}, dimensions={0} | all-to-all | bytes 524288 | tf_op jit(solution)/shard_map/all_to_all | solution.py:257
  67.9 0.0 copy-done
  67.9 19.1 %all_to_all.27.early_ref = bf16[32,32,256]{2,1,0:T(8,128)(2,1)} all-to-all(bf16[32,32,256]{2,1,0:T(8,128)(2,1)S(1)} %bitcast.3), channel_id=1, replica_groups=mesh['row'=32,'feat'=8] {'row'}, dimensions={0} | all-to-all | bytes 1048576 | tf_op jit(solution)/shard_map/all_to_all | solution.py:257
  87.0 2.3 %gains.1 = f32[32,8,128]{2,1,0:T(8,128)} custom-call(bf16[32,32,256]{2,1,0:T(8,128)(2,1)} %all_to_all.27.early_ref, bf16[32,16,256]{2,1,0:T(8,128)(2,1)} %all_to_all.26.late_ref), custom_call_target="tpu_custom_call" | custom-call | tf_op jit(solution)/shard_map/gains/pallas_call | solution.py:259
  89.4 17.6 %all_to_all.28.parts_ref = f32[32,8,128]{2,1,0:T(8,128)S(1)} all-to-all(f32[32,8,128]{2,1,0:T(8,128)} %gains.1), channel_id=1, replica_groups=mesh['row'=32,'feat'=8] {'row'}, dimensions={0} | all-to-all | bytes 262144 | tf_op jit(solution)/shard_map/all_to_all | solution.py:264
  107.0 0.0 copy-start.1
  107.0 0.6 broadcast_in_dim.2
  107.6 6.4 %all-to-all-start.4 = ((f32[8,8,128]{2,1,0:T(8,128)}), f32[8,8,128]{2,1,0:T(8,128)S(1)}, u32[]{:S(2)}, u32[]{:S(2)}) async-start(f32[8,8,128]{2,1,0:T(8,128)} %broadcast_in_dim.2), calls=%async_computation.4 | async-start | bytes 65536 | tf_op jit(solution)/shard_map/all_to_all | solution.py:266
  114.0 0.0 copy-done.1
  114.0 3.1 %children.1 = f32[8,8,384]{2,1,0:T(8,128)} custom-call(s32[8]{0:T(128)} %smaller_ref.3, f32[32,8,128]{2,1,0:T(8,128)} %copy-done.1, f32[8,8,192]{2,1,0:T(8,128)} %parent_ref.1), custom_call_target="tpu_custom_call" | custom-call | tf_op jit(solution)/shard_map/children/pallas_call | solution.py:267
  117.2 1.6 %all-to-all-done.4 = f32[8,8,128]{2,1,0:T(8,128)S(1)} async-done(((f32[8,8,128]{2,1,0:T(8,128)}), f32[8,8,128]{2,1,0:T(8,128)S(1)}, u32[]{:S(2)}, u32[]{:S(2)}) %all-to-all-start.4) | async-done | bytes 32800 | tf_op jit(solution)/shard_map/all_to_all | solution.py:266
  118.8 0.6 slice_bitcast_fusion
  (2 shorter events, 0.0 us)
Async XLA Ops:
  39.4 28.5 %copy-start = (bf16[64,16,256]{2,1,0:T(8,128)(2,1)S(1)}, bf16[64,16,256]{2,1,0:T(8,128)(2,1)}, u32[]{:S(2)}) copy-start(bf16[64,16,256]{2,1,0:T(8,128)(2,1)} %histograms.2.after_ref) | copy-start | bytes 1572868
  107.0 7.1 %copy-start.1 = (f32[32,8,128]{2,1,0:T(8,128)}, f32[32,8,128]{2,1,0:T(8,128)S(1)}, u32[]{:S(2)}) copy-start(f32[32,8,128]{2,1,0:T(8,128)S(1)} %all_to_all.28.parts_ref) | copy-start | bytes 393220
  107.6 11.2 %all-to-all-start.4 = ((f32[8,8,128]{2,1,0:T(8,128)}), f32[8,8,128]{2,1,0:T(8,128)S(1)}, u32[]{:S(2)}, u32[]{:S(2)}) async-start(f32[8,8,128]{2,1,0:T(8,128)} %broadcast_in_dim.2), calls=%async_computation.4 | async-start | bytes 65536 | tf_op jit(solution)/shard_map/all_to_all | solution.py:266

commit v3 on v2

--- a/solution.py
+++ b/solution.py
@@ -8,7 +8,11 @@
 levels = 5
 reg_lambda = 1.0
 SHARE = 128
-EARLY = 2
+HIGHS = 4
+LOWS = 256 // HIGHS
+CHUNK = 512
+BLOCK = 256
+FEATS = 96
 
 
 def node_column(smaller_ref, parents):
@@ -102,72 +106,157 @@
     )(counts, scores, labels)
 
 
-def weight_kernel(smaller_ref, lam_ref, child_ref, weight_ref):
-    query_dev, slots = child_ref.shape
+def prefix_lanes(values):
+    lane = lax.broadcasted_iota(jnp.int32, values.shape, 1)
+    step = 1
+    while step < values.shape[1]:
+        values = values + jnp.where(lane >= step, pltpu.roll(values, step, 1), 0.0)
+        step *= 2
+    return values
+
+
+def compact(smaller_ref, counts_ref, lam_ref, child_ref, codes_ref, high_ref, low_ref, weight_ref, chunks_ref):
+    query_dev, feats, slots = codes_ref.shape
     parents = smaller_ref.shape[0]
-    nodes = 2 * lax.broadcasted_iota(jnp.int32, (parents, 1), 0) + node_column(smaller_ref, parents)
+    lane = lax.broadcasted_iota(jnp.int32, (1, slots), 1)
     lam = jnp.concatenate([lam_ref[k].astype(jnp.float32) for k in range(lam_ref.shape[0])], axis=1)
+    child = child_ref[...]
+    parent = child >> 1
+    wanted = jnp.zeros_like(child)
+    for p in range(parents):
+        wanted = jnp.where(parent == p, smaller_ref[p], wanted)
+    usable = jnp.concatenate([(lane < counts_ref[q]).astype(jnp.int32) for q in range(query_dev)], axis=0) > 0
+    live = ((child & 1) == wanted) & usable
+    mine = live.astype(jnp.float32)
+    rank = prefix_lanes(mine) - mine
+    starts = []
+    first = jnp.int32(0)
     for q in range(query_dev):
-        member = child_ref[q : q + 1, :] == nodes
+        starts.append([])
+        for at in range(0, slots, BLOCK):
+            starts[q].append(first)
+            first = first + jnp.sum(mine[q : q + 1, at : at + BLOCK]).astype(jnp.int32)
+    chunks = (first + CHUNK - 1) // CHUNK
+    chunks_ref[0] = chunks
+
+    def clear(t, carry):
+        at = pl.ds(pl.multiple_of(t * CHUNK, CHUNK), CHUNK)
+        low_ref[:, at] = jnp.zeros((feats, CHUNK), jnp.float32)
+        weight_ref[:, at] = jnp.zeros((16, CHUNK), jnp.float32)
+        return carry
+
+    lax.fori_loop(0, chunks + 1, clear, 0)
+    window = BLOCK + 128
+    mark = lax.broadcasted_iota(jnp.int32, (window, 1), 0).astype(jnp.float32)
+    one = jnp.ones((), jnp.bfloat16)
+    zero = jnp.zeros((), jnp.bfloat16)
+    local = lax.broadcasted_iota(jnp.int32, (parents, 1), 0)
+    for q in range(query_dev):
+        member = (parent[q : q + 1] == local) & live[q : q + 1]
         grad = jnp.where(member, lam[q : q + 1], 0.0)
         hess = jnp.where(member, lam[8 + q : 9 + q], 0.0)
-        weight_ref[:, q * slots : (q + 1) * slots] = jnp.concatenate((grad, hess), axis=0).astype(jnp.bfloat16)
-
-
-def histogram_kernel(codes_ref, weight_ref, after_ref, hist_ref):
-    del after_ref
-    query_dev, feats, slots = codes_ref.shape
+        rows = jnp.concatenate((grad, hess), axis=0)
+        moved = jnp.concatenate((codes_ref[q].astype(jnp.float32).astype(jnp.bfloat16), rows.astype(jnp.bfloat16)), axis=0)
+        spot = jnp.where(live[q : q + 1], rank[q : q + 1] + starts[q][0].astype(jnp.float32), -1.0)
+        for k, begin in enumerate(starts[q]):
+            to = pl.multiple_of((begin // 128) * 128, 128)
+            block = slice(k * BLOCK, (k + 1) * BLOCK)
+            hot = jnp.where(spot[:, block] - to.astype(jnp.float32) == mark, one, zero)
+            here = lax.dot_general(
+                moved[:, block], hot, (((1,), (1,)), ((), ())), preferred_element_type=jnp.float32
+            )
+            low_ref[:, pl.ds(to, window)] += here[:feats]
+            weight_ref[:, pl.ds(to, window)] += here[feats:]
+
+    def split(t, carry):
+        at = pl.ds(pl.multiple_of(t * CHUNK, CHUNK), CHUNK)
+        code = low_ref[:, at]
+        high = jnp.floor(code * (1.0 / LOWS))
+        high_ref[:, at] = high
+        low_ref[:, at] = code - high * LOWS
+        return carry
+
+    lax.fori_loop(0, chunks, split, 0)
+
+
+def histogram_kernel(
+    smaller_ref, counts_ref, lam_ref, child_ref, codes_ref, hist_ref,
+    high_ref, low_ref, weight_ref, acc_ref, chunks_ref,
+):
+    feats = hist_ref.shape[0]
+
+    @pl.when(pl.program_id(0) == 0)
+    def _():
+        compact(
+            smaller_ref, counts_ref, lam_ref, child_ref, codes_ref,
+            high_ref, low_ref, weight_ref, chunks_ref,
+        )
+
     one = jnp.ones((), jnp.bfloat16)
     zero = jnp.zeros((), jnp.bfloat16)
-    low_mark = lax.broadcasted_iota(jnp.int32, (64, 1), 0).astype(jnp.float32).astype(jnp.bfloat16)
-    for group in range(feats // 4):
-        total = jnp.zeros((256, 256), jnp.float32)
-        for q in range(query_dev):
-            weight = weight_ref[:, q * slots : (q + 1) * slots]
+    low_mark = lax.broadcasted_iota(jnp.int32, (LOWS, 1), 0).astype(jnp.float32).astype(jnp.bfloat16)
+    base = pl.multiple_of(pl.program_id(0) * feats, 8)
+    acc_ref[...] = jnp.zeros_like(acc_ref)
+
+    def chunk(t, carry):
+        at = pl.ds(pl.multiple_of(t * CHUNK, CHUNK), CHUNK)
+        weight = weight_ref[:, at].astype(jnp.bfloat16)
+        high_rows = high_ref[pl.ds(base, feats), at]
+        low_rows = low_ref[pl.ds(base, feats), at]
+        for part in range(feats // HIGHS):
             lhs = []
             rhs = []
-            for f in range(4 * group, 4 * group + 4):
-                code = codes_ref[q, f : f + 1, :]
-                high = jnp.broadcast_to((code >> 6).astype(jnp.float32), (16, slots)).astype(jnp.bfloat16)
-                low = jnp.broadcast_to((code & 63).astype(jnp.float32), (64, slots)).astype(jnp.bfloat16)
-                for h in range(4):
+            for f in range(part * HIGHS, part * HIGHS + HIGHS):
+                high = jnp.broadcast_to(high_rows[f : f + 1], (16, CHUNK)).astype(jnp.bfloat16)
+                low = jnp.broadcast_to(low_rows[f : f + 1], (LOWS, CHUNK)).astype(jnp.bfloat16)
+                for h in range(HIGHS):
                     lhs.append(jnp.where(high == jnp.asarray(h, jnp.bfloat16), weight, zero))
                 rhs.append(jnp.where(low == low_mark, one, zero))
-            total += lax.dot_general(
+            acc_ref[part] += lax.dot_general(
                 jnp.concatenate(lhs, axis=0), jnp.concatenate(rhs, axis=0),
                 (((1,), (1,)), ((), ())), preferred_element_type=jnp.float32,
             )
-        for k in range(4):
-            pieces = [total[k * 64 + h * 16 : k * 64 + h * 16 + 16, k * 64 : k * 64 + 64] for h in range(4)]
-            hist_ref[4 * group + k] = jnp.concatenate(pieces, axis=1).astype(jnp.bfloat16)
-
-
-def histograms(bin_codes, weight, after, first, count):
+        return carry
+
+    lax.fori_loop(0, chunks_ref[0], chunk, 0)
+    wide = HIGHS * 16
+    for f in range(feats):
+        part, k = f // HIGHS, f % HIGHS
+        pieces = [
+            acc_ref[part, k * wide + h * 16 : k * wide + (h + 1) * 16, k * LOWS : (k + 1) * LOWS]
+            for h in range(HIGHS)
+        ]
+        hist_ref[f] = jnp.concatenate(pieces, axis=1).astype(jnp.bfloat16)
+
+
+def histograms(smaller, counts, lam, row_child, bin_codes):
     query_dev, feat_dev, slots = bin_codes.shape
+    room = query_dev * slots + CHUNK
+    smem = pl.BlockSpec(memory_space=pltpu.SMEM)
+
+    def whole(array):
+        return pl.BlockSpec(array.shape, lambda i: (0,) * array.ndim, pipeline_mode=pl.Buffered(1))
+
     return pl.pallas_call(
         histogram_kernel,
-        grid=(count // 8,),
-        out_shape=jax.ShapeDtypeStruct((count, 16, 256), jnp.bfloat16),
-        in_specs=[
-            pl.BlockSpec((query_dev, 8, slots), lambda i: (0, i + first // 8, 0)),
-            pl.BlockSpec(weight.shape, lambda i: (0, 0)),
-            pl.BlockSpec(memory_space=pl.ANY),
+        grid=(feat_dev // FEATS,),
+        out_shape=jax.ShapeDtypeStruct((feat_dev, 16, 256), jnp.bfloat16),
+        in_specs=[smem, smem, whole(lam), whole(row_child), whole(bin_codes)],
+        out_specs=pl.BlockSpec((FEATS, 16, 256), lambda i: (i, 0, 0)),
+        scratch_shapes=[
+            pltpu.VMEM((feat_dev, room), jnp.float32),
+            pltpu.VMEM((feat_dev, room), jnp.float32),
+            pltpu.VMEM((16, room), jnp.float32),
+            pltpu.VMEM((FEATS // HIGHS, HIGHS * HIGHS * 16, 256), jnp.float32),
+            pltpu.SMEM((1,), jnp.int32),
         ],
-        out_specs=pl.BlockSpec((8, 16, 256), lambda i: (i, 0, 0)),
         name="histograms",
-    )(bin_codes, weight, after)
-
-
-def gain_kernel(early_ref, late_ref, send_ref):
-    rows = early_ref.shape[1] + late_ref.shape[1]
-    bins = early_ref.shape[2]
-    built = jnp.concatenate(
-        (
-            jnp.sum(early_ref[...].astype(jnp.float32), axis=0),
-            jnp.sum(late_ref[...].astype(jnp.float32), axis=0),
-        ),
-        axis=0,
-    )
+    )(smaller, counts, lam, row_child, bin_codes)
+
+
+def gain_kernel(parts_ref, send_ref):
+    rows, bins = parts_ref.shape[1:]
+    built = jnp.sum(parts_ref[...].astype(jnp.float32), axis=0)
     below = lax.broadcasted_iota(jnp.int32, (bins, bins), 0)
     upto = lax.broadcasted_iota(jnp.int32, (bins, bins), 1)
     left = jnp.dot(
@@ -199,22 +288,13 @@
     sources, bin_span, lanes = parts_ref.shape
     parents, width = children_ref.shape[1:]
     group = width // sources
-    early = EARLY * sources
-
-    def place(column):
-        feat = column // 4
-        is_early = feat < early
-        owner = jnp.where(is_early, feat // EARLY, (feat - early) % sources)
-        local = jnp.where(is_early, feat % EARLY, EARLY + (feat - early) // sources)
-        return owner, local
-
     column = lax.broadcasted_iota(jnp.int32, (sources, width), 1)
     source = lax.broadcasted_iota(jnp.int32, (sources, width), 0)
-    spread = (place(column)[0] == source).astype(jnp.float32)
+    spread = (column // group == source).astype(jnp.float32)
     rows = group * parents // 2
     row = lax.broadcasted_iota(jnp.int32, (rows, width), 0)
     col = lax.broadcasted_iota(jnp.int32, (rows, width), 1)
-    match = (row // (2 * parents) == place(col)[1]) & ((row // parents) % 2 == col % 2)
+    match = (row // (2 * parents) == (col % group) // 4) & ((row // parents) % 2 == col % 2)
     pick_row = lax.broadcasted_iota(jnp.int32, (width // 2, width), 0)
     pick_col = lax.broadcasted_iota(jnp.int32, (width // 2, width), 1)
     pick = (pick_row == (pick_col // 4) * 2 + pick_col % 2).astype(jnp.float32)
@@ -244,23 +324,13 @@
     vmem = pl.BlockSpec(memory_space=pltpu.VMEM)
     smem = pl.BlockSpec(memory_space=pltpu.SMEM)
     lam = lax.all_to_all(lambdas(scores, labels, counts), "feat", 0, 0, tiled=True)
-    weight = pl.pallas_call(
-        weight_kernel,
-        out_shape=jax.ShapeDtypeStruct((2 * parents, row_child.size), jnp.bfloat16),
-        in_specs=[smem, vmem, vmem], out_specs=vmem, name="weights",
-    )(smaller, lam, row_child)
-    received = []
-    first, hist = 0, weight
-    for count in (EARLY * row_count, feat_dev - EARLY * row_count):
-        hist = histograms(bin_codes, weight, hist, first, count)
-        parts = hist.reshape(row_count, count // row_count * 2 * parents, bins)
-        received.append(lax.all_to_all(parts, "row", 0, 0, tiled=True))
-        first += count
+    hist = histograms(smaller, counts, lam, row_child, bin_codes)
+    parts = lax.all_to_all(hist.reshape(row_count, rows, bins), "row", 0, 0, tiled=True)
     send = pl.pallas_call(
         gain_kernel,
         out_shape=jax.ShapeDtypeStruct((row_count, bin_span, 128), jnp.float32),
-        in_specs=[vmem, vmem], out_specs=vmem, name="gains",
-    )(*received)
+        in_specs=[vmem], out_specs=vmem, name="gains",
+    )(parts)
     own = lax.all_to_all(send, "row", 0, 0, tiled=True)
     best = jnp.broadcast_to(jnp.max(own, axis=0)[None], (feat_count, bin_span, 128))
     best = jnp.max(lax.all_to_all(best, "feat", 0, 0, tiled=True), axis=0)

time: 120 us -> 99 us (0.82)
  Pallas kernels: 41.7 us -> 28.5 us
  blocking collectives: 67.8 us -> 60.6 us
    pallas_call x3 -> x1, Pallas kernels: 27.9 us -> 14.8 us  [histograms(): pl.pallas_call(histogram_kernel, grid=(feat_dev // FEATS,), out_shape=jax...]
    all_to_all x2 -> x1, blocking collectives: 38.2 us -> 31.4 us  [shards(): lax.all_to_all(hist.reshape(row_count, rows, bins), 'row', 0, 0, tiled=True)]
where the time goes in v3:
time: 99 us; the launch traced here: 98.5 us
  blocking collectives  60.6 us (61%)
  Pallas kernels  28.5 us (29%)
  starting transfers between devices  5.93 us (6%)
  waiting for transfers between devices  1.6 us (2%)
  local copies, waits for them, and re-layouts  1.2 us (1%)
    all_to_all x1, blocking collectives, shards(): lax.all_to_all(hist.reshape(row_count, rows, bins), 'row', 0, 0, tiled=True)  31.4 us
    all_to_all x1, blocking collectives, shards(): own = lax.all_to_all(send, 'row', 0, 0, tiled=True)  17.3 us
    pallas_call x1, Pallas kernels, histograms(): pl.pallas_call(histogram_kernel, grid=(feat_dev // FEATS,), out_shape=jax...  14.8 us
    all_to_all x1, blocking collectives, shards(): lax.all_to_all(lambdas(scores, labels, counts), 'feat', 0, 0, tiled=True)  11.8 us
    pallas_call x1, Pallas kernels, lambdas(): pl.pallas_call(lambda_kernel, out_shape=jax.ShapeDtypeStruct((slots // SH...  8.17 us
    all_to_all x1, starting transfers between devices, shards(): best = jnp.max(lax.all_to_all(best, 'feat', 0, 0, tiled=True), axis=0)  5.93 us
    pallas_call x1, Pallas kernels, shards(): pl.pallas_call(children_kernel, out_shape=jax.ShapeDtypeStruct((bin_span,...  3.14 us
    pallas_call x1, Pallas kernels, shards(): pl.pallas_call(gain_kernel, out_shape=jax.ShapeDtypeStruct((row_count, bi...  2.35 us
  transfers between devices with their start and end apart: 1, of which 1 were waited for; matrix products, arithmetic and copies ran while one was open for 0% of the time, Pallas kernels for 3%

profile of v3, /device:TPU:1, one launch (start us, length us, event | category | flops | bytes accessed | tf_op | source)
XLA Modules:
  0.0 98.5 jit_solution(8965500844534217461)
XLA Ops:
  0.6 8.2 %lambdas.1 = bf16[8,16,128]{2,1,0:T(8,128)(2,1)} custom-call(s32[6]{0:T(128)} %counts_ref.3, f32[6,1024]{1,0:T(8,128)} %scores_ref.1, s32[6,1024]{1,0:T(8,128)} %labels_ref.1), custom_call_target="tpu_custom_call" | custom-call | tf_op jit(solution)/shard_map/lambdas/pallas_call | solution.py:99
  8.8 11.8 %all_to_all.20.lam_ref = bf16[8,16,128]{2,1,0:T(8,128)(2,1)} all-to-all(bf16[8,16,128]{2,1,0:T(8,128)(2,1)} %lambdas.1), channel_id=1, replica_groups=mesh['row'=32,'feat'=8] {'feat'}, dimensions={0} | all-to-all | bytes 65536 | tf_op jit(solution)/shard_map/all_to_all | solution.py:326
  20.6 14.8 %histograms.1 = bf16[96,16,256]{2,1,0:T(8,128)(2,1)} custom-call(s32[8]{0:T(128)} %smaller_ref.3, s32[6]{0:T(128)} %counts_ref.3, bf16[8,16,128]{2,1,0:T(8,128)(2,1)} %all_to_all.20.lam_ref, s32[6,1024]{1,0:T(8,128)} %child_ref.1, s32[6,96,1024]{2,1,0:T(8,128)} %codes_ref.1), custom_call_target="tpu_custom_call" | custom-call | tf_op jit(solution)/shard_map/histograms/pallas_call | solution.py:240
  35.5 31.4 %all_to_all.21.parts_ref = bf16[32,48,256]{2,1,0:T(8,128)(2,1)} all-to-all(bf16[32,48,256]{2,1,0:T(8,128)(2,1)} %bitcast.3), channel_id=1, replica_groups=mesh['row'=32,'feat'=8] {'row'}, dimensions={0} | all-to-all | bytes 1572864 | tf_op jit(solution)/shard_map/all_to_all | solution.py:328
  66.9 2.4 %gains.1 = f32[32,8,128]{2,1,0:T(8,128)} custom-call(bf16[32,48,256]{2,1,0:T(8,128)(2,1)} %all_to_all.21.parts_ref), custom_call_target="tpu_custom_call" | custom-call | tf_op jit(solution)/shard_map/gains/pallas_call | solution.py:329
  69.2 17.3 %all_to_all.22.parts_ref = f32[32,8,128]{2,1,0:T(8,128)S(1)} all-to-all(f32[32,8,128]{2,1,0:T(8,128)} %gains.1), channel_id=1, replica_groups=mesh['row'=32,'feat'=8] {'row'}, dimensions={0} | all-to-all | bytes 262144 | tf_op jit(solution)/shard_map/all_to_all | solution.py:334
  86.5 0.0 copy-start
  86.6 0.6 broadcast_in_dim.2
  87.2 5.9 %all-to-all-start.3 = ((f32[8,8,128]{2,1,0:T(8,128)}), f32[8,8,128]{2,1,0:T(8,128)S(1)}, u32[]{:S(2)}, u32[]{:S(2)}) async-start(f32[8,8,128]{2,1,0:T(8,128)} %broadcast_in_dim.2), calls=%async_computation.3 | async-start | bytes 65536 | tf_op jit(solution)/shard_map/all_to_all | solution.py:336
  93.1 0.0 copy-done
  93.1 3.1 %children.1 = f32[8,8,384]{2,1,0:T(8,128)} custom-call(s32[8]{0:T(128)} %smaller_ref.3, f32[32,8,128]{2,1,0:T(8,128)} %copy-done, f32[8,8,192]{2,1,0:T(8,128)} %parent_ref.1), custom_call_target="tpu_custom_call" | custom-call | tf_op jit(solution)/shard_map/children/pallas_call | solution.py:337
  96.3 1.6 %all-to-all-done.3 = f32[8,8,128]{2,1,0:T(8,128)S(1)} async-done(((f32[8,8,128]{2,1,0:T(8,128)}), f32[8,8,128]{2,1,0:T(8,128)S(1)}, u32[]{:S(2)}, u32[]{:S(2)}) %all-to-all-start.3) | async-done | bytes 32800 | tf_op jit(solution)/shard_map/all_to_all | solution.py:336
  97.9 0.6 slice_bitcast_fusion
  (2 shorter events, 0.0 us)
Async XLA Ops:
  86.5 6.6 %copy-start = (f32[32,8,128]{2,1,0:T(8,128)}, f32[32,8,128]{2,1,0:T(8,128)S(1)}, u32[]{:S(2)}) copy-start(f32[32,8,128]{2,1,0:T(8,128)S(1)} %all_to_all.22.parts_ref) | copy-start | bytes 393220
  87.2 10.7 %all-to-all-start.3 = ((f32[8,8,128]{2,1,0:T(8,128)}), f32[8,8,128]{2,1,0:T(8,128)S(1)}, u32[]{:S(2)}, u32[]{:S(2)}) async-start(f32[8,8,128]{2,1,0:T(8,128)} %broadcast_in_dim.2), calls=%async_computation.3 | async-start | bytes 65536 | tf_op jit(solution)/shard_map/all_to_all | solution.py:336

commit v4 on v3

--- a/solution.py
+++ b/solution.py
@@ -8,6 +8,7 @@
 levels = 5
 reg_lambda = 1.0
 SHARE = 128
+STRETCH = 1024
 HIGHS = 4
 LOWS = 256 // HIGHS
 CHUNK = 512
@@ -23,85 +24,87 @@
     return column
 
 
-def lambda_kernel(
-    counts_ref, scores_ref, labels_ref, lam_ref,
-    exp_row, gain_row, disc_row, exp_col, gain_col, disc_col, lam_rows,
-):
+def count_column(counts_ref):
+    which = lax.broadcasted_iota(jnp.int32, (8, 1), 0)
+    column = jnp.zeros((8, 1), jnp.int32)
+    for q in range(counts_ref.shape[0]):
+        column = jnp.where(which == q, counts_ref[q], column)
+    return column
+
+
+def lambda_kernel(counts_ref, scores_ref, labels_ref, lam_ref, rows_ref, cols_ref, sums_ref):
     query_dev, slots = scores_ref.shape
     own = pl.multiple_of(lax.axis_index("feat") * SHARE, SHARE)
-    position = lax.broadcasted_iota(jnp.int32, (1, slots), 1)
+    position = lax.broadcasted_iota(jnp.int32, (8, slots), 1)
     discount = 1.0 / jnp.log2(position.astype(jnp.float32) + 2.0)
-    disc_row[...] = jnp.broadcast_to(discount, (8, slots))
-    exp_row[...] = jnp.zeros_like(exp_row)
-    gain_row[...] = jnp.zeros_like(gain_row)
-    lam_rows[...] = jnp.zeros_like(lam_rows)
-    score_exp = jnp.exp(scores_ref[...])
-    rel_gain = jnp.exp2(labels_ref[...].astype(jnp.float32)) - 1.0
-    for q in range(query_dev):
-        usable = position < counts_ref[q]
-        exp_row[q : q + 1, :] = jnp.where(usable, score_exp[q : q + 1], 0.0)
-        gain_row[q : q + 1, :] = jnp.where(usable, rel_gain[q : q + 1], -1.0)
-    exp_col[...] = exp_row[...].T
-    gain_col[...] = gain_row[...].T
-    disc_col[...] = disc_row[...].T
+    counts = count_column(counts_ref)
+    grade = labels_ref[...]
+    usable = position[:query_dev] < counts[:query_dev]
+    rows_ref[0:16, :] = jnp.zeros((16, slots), jnp.float32)
+    rows_ref[0:query_dev, :] = jnp.where(usable, jnp.exp(scores_ref[...]), 0.0)
+    rows_ref[8 : 8 + query_dev, :] = jnp.where(usable, jnp.exp2(grade.astype(jnp.float32)) - 1.0, -1.0)
+    rows_ref[16:24, :] = discount
+    cols_ref[...] = rows_ref[...].T
+    sums_ref[...] = jnp.zeros_like(sums_ref)
+
+    ideal = jnp.zeros((query_dev, slots), jnp.float32)
+    ahead = jnp.zeros((query_dev, 1), jnp.int32)
+    for c in range(levels - 1, 0, -1):
+        here = jnp.sum(((grade == c) & usable).astype(jnp.float32), axis=1, keepdims=True).astype(jnp.int32)
+        span = (position[:query_dev] >= ahead) & (position[:query_dev] < ahead + here)
+        ideal = ideal + jnp.where(span, float(2**c - 1), 0.0)
+        ahead = ahead + here
+    ideal = jnp.sum(ideal * discount[:query_dev], axis=1, keepdims=True)
+    inv_ideal = 1.0 / jnp.maximum(ideal, 1.0)
 
     for q in range(query_dev):
         count = counts_ref[q]
-        e_i = exp_row[q : q + 1, pl.ds(own, SHARE)]
-        g_i = gain_row[q : q + 1, pl.ds(own, SHARE)]
-        d_i = disc_row[0:1, pl.ds(own, SHARE)]
+        e_i = rows_ref[q : q + 1, pl.ds(own, SHARE)]
+        g_i = rows_ref[8 + q : 9 + q, pl.ds(own, SHARE)]
+        d_i = rows_ref[16:17, pl.ds(own, SHARE)]
 
         def partners(jb, sums, q=q, e_i=e_i, g_i=g_i, d_i=d_i):
             grad_sum, hess_sum = sums
-            at = pl.multiple_of(jb * 128, 128)
-            e_j = exp_col[pl.ds(at, 128), q : q + 1]
-            g_j = gain_col[pl.ds(at, 128), q : q + 1]
-            d_j = disc_col[pl.ds(at, 128), 0:1]
+            at = pl.ds(pl.multiple_of(jb * STRETCH, STRETCH), STRETCH)
+            e_j = cols_ref[at, q : q + 1]
+            g_j = cols_ref[at, 8 + q : 9 + q]
+            d_j = cols_ref[at, 16:17]
             inverse = 1.0 / (e_i + e_j)
             gain_gap = g_i - g_j
             higher = gain_gap > 0.0
             part = gain_gap * (jnp.abs(d_i - d_j) * inverse)
             grad = part * jnp.where(higher, e_j, e_i)
             hess = jnp.abs(grad) * (inverse * jnp.where(higher, e_i, e_j))
-            grad_sum = grad_sum + jnp.sum(grad.reshape(16, 8, SHARE), axis=0)
-            hess_sum = hess_sum + jnp.sum(hess.reshape(16, 8, SHARE), axis=0)
+            grad_sum = grad_sum + jnp.sum(grad.reshape(STRETCH // 32, 32, SHARE), axis=0)
+            hess_sum = hess_sum + jnp.sum(hess.reshape(STRETCH // 32, 32, SHARE), axis=0)
             return grad_sum, hess_sum
 
-        zero = jnp.zeros((8, SHARE), jnp.float32)
-        last = jnp.where(own < count, (count + 127) // 128, 0)
+        zero = jnp.zeros((32, SHARE), jnp.float32)
+        last = jnp.where(own < count, (count + STRETCH - 1) // STRETCH, 0)
         grad_sum, hess_sum = lax.fori_loop(0, last, partners, (zero, zero))
-
-        grade = labels_ref[q : q + 1, :]
-        usable = position < count
-        ideal = jnp.zeros((1, slots), jnp.float32)
-        ahead = jnp.zeros((1, 1), jnp.int32)
-        for c in range(levels - 1, 0, -1):
-            here = jnp.sum(((grade == c) & usable).astype(jnp.int32), axis=1, keepdims=True)
-            span = (position >= ahead) & (position < ahead + here)
-            ideal = ideal + jnp.where(span, float(2**c - 1), 0.0)
-            ahead = ahead + here
-        inv_ideal = 1.0 / jnp.maximum(jnp.sum(ideal * discount, axis=1, keepdims=True), 1.0)
-        mine = own + lax.broadcasted_iota(jnp.int32, (1, SHARE), 1) < count
-        grad = -jnp.sum(grad_sum, axis=0, keepdims=True) * inv_ideal
-        hess = jnp.sum(hess_sum, axis=0, keepdims=True) * inv_ideal
-        lam_rows[q : q + 1, :] = jnp.where(mine, grad, 0.0)
-        lam_rows[8 + q : 9 + q, :] = jnp.where(mine, hess, 0.0)
-
-    lam_ref[...] = jnp.broadcast_to(lam_rows[...].astype(jnp.bfloat16)[None], lam_ref.shape)
+        sums_ref[q : q + 1, :] = -jnp.sum(grad_sum, axis=0, keepdims=True)
+        sums_ref[8 + q : 9 + q, :] = jnp.sum(hess_sum, axis=0, keepdims=True)
+
+    mine = own + lax.broadcasted_iota(jnp.int32, (query_dev, SHARE), 1) < counts[:query_dev]
+    sums_ref[0:query_dev, :] = jnp.where(mine, sums_ref[0:query_dev, :] * inv_ideal, 0.0)
+    sums_ref[8 : 8 + query_dev, :] = jnp.where(mine, sums_ref[8 : 8 + query_dev, :] * inv_ideal, 0.0)
+    lam_ref[...] = jnp.broadcast_to(sums_ref[...].astype(jnp.bfloat16)[None], lam_ref.shape)
 
 
 def lambdas(scores, labels, counts):
     query_dev, slots = scores.shape
     vmem = pl.BlockSpec(memory_space=pltpu.VMEM)
     smem = pl.BlockSpec(memory_space=pltpu.SMEM)
-    row = pltpu.VMEM((8, slots), jnp.float32)
-    col = pltpu.VMEM((slots, 8), jnp.float32)
     return pl.pallas_call(
         lambda_kernel,
         out_shape=jax.ShapeDtypeStruct((slots // SHARE, 16, SHARE), jnp.bfloat16),
         in_specs=[smem, vmem, vmem],
         out_specs=vmem,
-        scratch_shapes=[row, row, row, col, col, col, pltpu.VMEM((16, SHARE), jnp.float32)],
+        scratch_shapes=[
+            pltpu.VMEM((24, slots), jnp.float32),
+            pltpu.VMEM((slots, 24), jnp.float32),
+            pltpu.VMEM((16, SHARE), jnp.float32),
+        ],
         name="lambdas",
     )(counts, scores, labels)
 

time: 99 us -> 95.2 us (0.962)
  Pallas kernels: 28.5 us -> 25.3 us
    pallas_call x1, Pallas kernels: 8.17 us -> 4.96 us  [lambdas(): pl.pallas_call(lambda_kernel, out_shape=jax.ShapeDtypeStruct((slots // SH...]
where the time goes in v4:
time: 95.2 us; the launch traced here: 94.8 us
  blocking collectives  60.1 us (63%)
  Pallas kernels  25.3 us (27%)
  starting transfers between devices  5.93 us (6%)
  waiting for transfers between devices  1.6 us (2%)
  local copies, waits for them, and re-layouts  1.2 us (1%)
    all_to_all x1, blocking collectives, shards(): lax.all_to_all(hist.reshape(row_count, rows, bins), 'row', 0, 0, tiled=True)  31 us
    all_to_all x1, blocking collectives, shards(): own = lax.all_to_all(send, 'row', 0, 0, tiled=True)  17.3 us
    pallas_call x1, Pallas kernels, histograms(): pl.pallas_call(histogram_kernel, grid=(feat_dev // FEATS,), out_shape=jax...  14.8 us
    all_to_all x1, blocking collectives, shards(): lax.all_to_all(lambdas(scores, labels, counts), 'feat', 0, 0, tiled=True)  11.8 us
    all_to_all x1, starting transfers between devices, shards(): best = jnp.max(lax.all_to_all(best, 'feat', 0, 0, tiled=True), axis=0)  5.93 us
    pallas_call x1, Pallas kernels, lambdas(): pl.pallas_call(lambda_kernel, out_shape=jax.ShapeDtypeStruct((slots // SH...  4.96 us
    pallas_call x1, Pallas kernels, shards(): pl.pallas_call(children_kernel, out_shape=jax.ShapeDtypeStruct((bin_span,...  3.14 us
    pallas_call x1, Pallas kernels, shards(): pl.pallas_call(gain_kernel, out_shape=jax.ShapeDtypeStruct((row_count, bi...  2.35 us
  transfers between devices with their start and end apart: 1, of which 1 were waited for; matrix products, arithmetic and copies ran while one was open for 0% of the time, Pallas kernels for 3%

profile of v4, /device:TPU:1, one launch (start us, length us, event | category | flops | bytes accessed | tf_op | source)
XLA Modules:
  0.0 94.8 jit_solution(6862196934509908643)
XLA Ops:
  0.6 5.0 %lambdas.1 = bf16[8,16,128]{2,1,0:T(8,128)(2,1)} custom-call(s32[6]{0:T(128)} %counts_ref.3, f32[6,1024]{1,0:T(8,128)} %scores_ref.1, s32[6,1024]{1,0:T(8,128)} %labels_ref.1), custom_call_target="tpu_custom_call" | custom-call | tf_op jit(solution)/shard_map/lambdas/pallas_call | solution.py:98
  5.6 11.8 %all_to_all.20.lam_ref = bf16[8,16,128]{2,1,0:T(8,128)(2,1)} all-to-all(bf16[8,16,128]{2,1,0:T(8,128)(2,1)} %lambdas.1), channel_id=1, replica_groups=mesh['row'=32,'feat'=8] {'feat'}, dimensions={0} | all-to-all | bytes 65536 | tf_op jit(solution)/shard_map/all_to_all | solution.py:329
  17.4 14.8 %histograms.1 = bf16[96,16,256]{2,1,0:T(8,128)(2,1)} custom-call(s32[8]{0:T(128)} %smaller_ref.3, s32[6]{0:T(128)} %counts_ref.3, bf16[8,16,128]{2,1,0:T(8,128)(2,1)} %all_to_all.20.lam_ref, s32[6,1024]{1,0:T(8,128)} %child_ref.1, s32[6,96,1024]{2,1,0:T(8,128)} %codes_ref.1), custom_call_target="tpu_custom_call" | custom-call | tf_op jit(solution)/shard_map/histograms/pallas_call | solution.py:243
  32.3 31.0 %all_to_all.21.parts_ref = bf16[32,48,256]{2,1,0:T(8,128)(2,1)} all-to-all(bf16[32,48,256]{2,1,0:T(8,128)(2,1)} %bitcast.3), channel_id=1, replica_groups=mesh['row'=32,'feat'=8] {'row'}, dimensions={0} | all-to-all | bytes 1572864 | tf_op jit(solution)/shard_map/all_to_all | solution.py:331
  63.2 2.4 %gains.1 = f32[32,8,128]{2,1,0:T(8,128)} custom-call(bf16[32,48,256]{2,1,0:T(8,128)(2,1)} %all_to_all.21.parts_ref), custom_call_target="tpu_custom_call" | custom-call | tf_op jit(solution)/shard_map/gains/pallas_call | solution.py:332
  65.6 17.3 %all_to_all.22.parts_ref = f32[32,8,128]{2,1,0:T(8,128)S(1)} all-to-all(f32[32,8,128]{2,1,0:T(8,128)} %gains.1), channel_id=1, replica_groups=mesh['row'=32,'feat'=8] {'row'}, dimensions={0} | all-to-all | bytes 262144 | tf_op jit(solution)/shard_map/all_to_all | solution.py:337
  82.9 0.0 copy-start
  82.9 0.6 broadcast_in_dim.2
  83.5 5.9 %all-to-all-start.3 = ((f32[8,8,128]{2,1,0:T(8,128)}), f32[8,8,128]{2,1,0:T(8,128)S(1)}, u32[]{:S(2)}, u32[]{:S(2)}) async-start(f32[8,8,128]{2,1,0:T(8,128)} %broadcast_in_dim.2), calls=%async_computation.3 | async-start | bytes 65536 | tf_op jit(solution)/shard_map/all_to_all | solution.py:339
  89.5 0.0 copy-done
  89.5 3.1 %children.1 = f32[8,8,384]{2,1,0:T(8,128)} custom-call(s32[8]{0:T(128)} %smaller_ref.3, f32[32,8,128]{2,1,0:T(8,128)} %copy-done, f32[8,8,192]{2,1,0:T(8,128)} %parent_ref.1), custom_call_target="tpu_custom_call" | custom-call | tf_op jit(solution)/shard_map/children/pallas_call | solution.py:340
  92.6 1.6 %all-to-all-done.3 = f32[8,8,128]{2,1,0:T(8,128)S(1)} async-done(((f32[8,8,128]{2,1,0:T(8,128)}), f32[8,8,128]{2,1,0:T(8,128)S(1)}, u32[]{:S(2)}, u32[]{:S(2)}) %all-to-all-start.3) | async-done | bytes 32800 | tf_op jit(solution)/shard_map/all_to_all | solution.py:339
  94.2 0.6 slice_bitcast_fusion
  (2 shorter events, 0.0 us)
Async XLA Ops:
  82.9 6.6 %copy-start = (f32[32,8,128]{2,1,0:T(8,128)}, f32[32,8,128]{2,1,0:T(8,128)S(1)}, u32[]{:S(2)}) copy-start(f32[32,8,128]{2,1,0:T(8,128)S(1)} %all_to_all.22.parts_ref) | copy-start | bytes 393220
  83.5 10.7 %all-to-all-start.3 = ((f32[8,8,128]{2,1,0:T(8,128)}), f32[8,8,128]{2,1,0:T(8,128)S(1)}, u32[]{:S(2)}, u32[]{:S(2)}) async-start(f32[8,8,128]{2,1,0:T(8,128)} %broadcast_in_dim.2), calls=%async_computation.3 | async-start | bytes 65536 | tf_op jit(solution)/shard_map/all_to_all | solution.py:339

commit v5 on v4

--- a/solution.py
+++ b/solution.py
@@ -9,11 +9,11 @@
 reg_lambda = 1.0
 SHARE = 128
 STRETCH = 1024
-HIGHS = 4
+GROUPS = 4
+HIGHS = 8
 LOWS = 256 // HIGHS
-CHUNK = 512
-BLOCK = 256
-FEATS = 96
+CHUNK = 256
+BLOCK = 512
 
 
 def node_column(smaller_ref, parents):
@@ -118,29 +118,53 @@
     return values
 
 
-def compact(smaller_ref, counts_ref, lam_ref, child_ref, codes_ref, high_ref, low_ref, weight_ref, chunks_ref):
+def compact(
+    smaller_ref, counts_ref, lam_ref, child_ref, codes_ref,
+    high_ref, low_ref, weight_ref, moved_ref, spot_ref, chunks_ref,
+):
     query_dev, feats, slots = codes_ref.shape
     parents = smaller_ref.shape[0]
-    lane = lax.broadcasted_iota(jnp.int32, (1, slots), 1)
+    per_group = parents // GROUPS
+    blocks = slots // BLOCK
     lam = jnp.concatenate([lam_ref[k].astype(jnp.float32) for k in range(lam_ref.shape[0])], axis=1)
     child = child_ref[...]
     parent = child >> 1
     wanted = jnp.zeros_like(child)
     for p in range(parents):
         wanted = jnp.where(parent == p, smaller_ref[p], wanted)
-    usable = jnp.concatenate([(lane < counts_ref[q]).astype(jnp.int32) for q in range(query_dev)], axis=0) > 0
+    position = lax.broadcasted_iota(jnp.int32, child.shape, 1)
+    usable = position < count_column(counts_ref)[:query_dev]
     live = ((child & 1) == wanted) & usable
-    mine = live.astype(jnp.float32)
-    rank = prefix_lanes(mine) - mine
-    starts = []
-    first = jnp.int32(0)
-    for q in range(query_dev):
-        starts.append([])
-        for at in range(0, slots, BLOCK):
-            starts[q].append(first)
-            first = first + jnp.sum(mine[q : q + 1, at : at + BLOCK]).astype(jnp.int32)
-    chunks = (first + CHUNK - 1) // CHUNK
-    chunks_ref[0] = chunks
+    owner = jnp.where(live, parent // per_group, -1)
+    numbers = {}
+    ranks = []
+    for g in range(0, GROUPS, 2):
+        pair = jnp.where(owner == g, 1, jnp.where(owner == g + 1, 4096, 0)).astype(jnp.float32)
+        for q in range(query_dev):
+            for k in range(blocks):
+                total = jnp.sum(pair[q : q + 1, k * BLOCK : (k + 1) * BLOCK]).astype(jnp.int32)
+                numbers[g, q, k] = total & 4095
+                numbers[g + 1, q, k] = total >> 12
+        packed = (prefix_lanes(pair) - pair).astype(jnp.int32)
+        ranks += [(packed & 4095).astype(jnp.float32), (packed >> 12).astype(jnp.float32)]
+    starts = {}
+    base = jnp.int32(0)
+    crowded = jnp.int32(0)
+    which = lax.broadcasted_iota(jnp.int32, (8, 1), 0)
+    for g in range(GROUPS):
+        first = base
+        opening = jnp.zeros((8, 1), jnp.float32)
+        for q in range(query_dev):
+            opening = jnp.where(which == q, first.astype(jnp.float32), opening)
+            for k in range(blocks):
+                starts[g, q, k] = first
+                first = first + numbers[g, q, k]
+                crowded = jnp.maximum(crowded, numbers[g, q, k])
+        spot_ref[g, 0:query_dev, :] = jnp.where(owner == g, ranks[g] + opening[:query_dev], -1.0)
+        chunks = (first - base + CHUNK - 1) // CHUNK
+        chunks_ref[g, 0] = base // CHUNK
+        chunks_ref[g, 1] = chunks
+        base = base + chunks * CHUNK
 
     def clear(t, carry):
         at = pl.ds(pl.multiple_of(t * CHUNK, CHUNK), CHUNK)
@@ -148,28 +172,49 @@
         weight_ref[:, at] = jnp.zeros((16, CHUNK), jnp.float32)
         return carry
 
-    lax.fori_loop(0, chunks + 1, clear, 0)
-    window = BLOCK + 128
-    mark = lax.broadcasted_iota(jnp.int32, (window, 1), 0).astype(jnp.float32)
+    lax.fori_loop(0, base // CHUNK, clear, 0)
+    local = lax.broadcasted_iota(jnp.int32, (per_group, 1), 0)
+    for q in range(query_dev):
+        member = ((parent[q : q + 1] % per_group) == local) & live[q : q + 1]
+        grad = jnp.where(member, lam[q : q + 1], 0.0)
+        hess = jnp.where(member, lam[8 + q : 9 + q], 0.0)
+        rows = jnp.concatenate((grad, hess) * GROUPS, axis=0)
+        moved_ref[q, 0:feats, :] = codes_ref[q].astype(jnp.float32).astype(jnp.bfloat16)
+        moved_ref[q, feats : feats + 16, :] = rows.astype(jnp.bfloat16)
+    mark = lax.broadcasted_iota(jnp.int32, (128, 1), 0).astype(jnp.float32)
+    lane = lax.broadcasted_iota(jnp.int32, (1, 128), 1)
     one = jnp.ones((), jnp.bfloat16)
     zero = jnp.zeros((), jnp.bfloat16)
-    local = lax.broadcasted_iota(jnp.int32, (parents, 1), 0)
-    for q in range(query_dev):
-        member = (parent[q : q + 1] == local) & live[q : q + 1]
-        grad = jnp.where(member, lam[q : q + 1], 0.0)
-        hess = jnp.where(member, lam[8 + q : 9 + q], 0.0)
-        rows = jnp.concatenate((grad, hess), axis=0)
-        moved = jnp.concatenate((codes_ref[q].astype(jnp.float32).astype(jnp.bfloat16), rows.astype(jnp.bfloat16)), axis=0)
-        spot = jnp.where(live[q : q + 1], rank[q : q + 1] + starts[q][0].astype(jnp.float32), -1.0)
-        for k, begin in enumerate(starts[q]):
-            to = pl.multiple_of((begin // 128) * 128, 128)
-            block = slice(k * BLOCK, (k + 1) * BLOCK)
-            hot = jnp.where(spot[:, block] - to.astype(jnp.float32) == mark, one, zero)
-            here = lax.dot_general(
-                moved[:, block], hot, (((1,), (1,)), ((), ())), preferred_element_type=jnp.float32
-            )
-            low_ref[:, pl.ds(to, window)] += here[:feats]
-            weight_ref[:, pl.ds(to, window)] += here[feats:]
+
+    def place(skip):
+        for q in range(query_dev):
+            for k in range(blocks):
+                block = slice(k * BLOCK, (k + 1) * BLOCK)
+                moved = moved_ref[q, :, block]
+                for g in range(GROUPS):
+                    begin = starts[g, q, k]
+                    to = pl.multiple_of((begin // 128) * 128, 128)
+                    offset = begin - to
+                    ahead = spot_ref[g, q : q + 1, block] - (to + skip).astype(jnp.float32)
+                    shift = offset.astype(jnp.float32)
+                    here = jnp.where((ahead >= shift) & (ahead < shift + 128.0), ahead, -1.0)
+                    here = jnp.where(here >= 128.0, here - 128.0, here)
+                    hot = jnp.where(here == mark, one, zero)
+                    out = lax.dot_general(
+                        moved, hot, (((1,), (1,)), ((), ())), preferred_element_type=jnp.float32
+                    )
+                    now = jnp.where(lane >= offset, out, 0.0)
+                    then = jnp.where(lane >= offset, 0.0, out)
+                    for add, start in ((now, to + skip), (then, to + skip + 128)):
+                        at = pl.ds(pl.multiple_of(start, 128), 128)
+                        low_ref[:, at] += add[:feats]
+                        weight_ref[:, at] += add[feats:]
+
+    def turn(t, carry):
+        place(t * 128)
+        return carry
+
+    lax.fori_loop(0, (crowded + 127) // 128, turn, 0)
 
     def split(t, carry):
         at = pl.ds(pl.multiple_of(t * CHUNK, CHUNK), CHUNK)
@@ -179,87 +224,101 @@
         low_ref[:, at] = code - high * LOWS
         return carry
 
-    lax.fori_loop(0, chunks, split, 0)
+    lax.fori_loop(0, base // CHUNK, split, 0)
 
 
 def histogram_kernel(
     smaller_ref, counts_ref, lam_ref, child_ref, codes_ref, hist_ref,
-    high_ref, low_ref, weight_ref, acc_ref, chunks_ref,
+    high_ref, low_ref, weight_ref, moved_ref, spot_ref, acc_ref, chunks_ref,
 ):
     feats = hist_ref.shape[0]
-
-    @pl.when(pl.program_id(0) == 0)
-    def _():
-        compact(
-            smaller_ref, counts_ref, lam_ref, child_ref, codes_ref,
-            high_ref, low_ref, weight_ref, chunks_ref,
-        )
-
+    compact(
+        smaller_ref, counts_ref, lam_ref, child_ref, codes_ref,
+        high_ref, low_ref, weight_ref, moved_ref, spot_ref, chunks_ref,
+    )
+    kinds = 16 // GROUPS
+    wide = HIGHS * kinds
     one = jnp.ones((), jnp.bfloat16)
     zero = jnp.zeros((), jnp.bfloat16)
     low_mark = lax.broadcasted_iota(jnp.int32, (LOWS, 1), 0).astype(jnp.float32).astype(jnp.bfloat16)
-    base = pl.multiple_of(pl.program_id(0) * feats, 8)
+    slot = lax.broadcasted_iota(jnp.int32, (16, 1), 0) // kinds
+    lane = lax.broadcasted_iota(jnp.int32, (1, 128), 1)
     acc_ref[...] = jnp.zeros_like(acc_ref)
-
-    def chunk(t, carry):
-        at = pl.ds(pl.multiple_of(t * CHUNK, CHUNK), CHUNK)
-        weight = weight_ref[:, at].astype(jnp.bfloat16)
-        high_rows = high_ref[pl.ds(base, feats), at]
-        low_rows = low_ref[pl.ds(base, feats), at]
-        for part in range(feats // HIGHS):
-            lhs = []
-            rhs = []
-            for f in range(part * HIGHS, part * HIGHS + HIGHS):
-                high = jnp.broadcast_to(high_rows[f : f + 1], (16, CHUNK)).astype(jnp.bfloat16)
-                low = jnp.broadcast_to(low_rows[f : f + 1], (LOWS, CHUNK)).astype(jnp.bfloat16)
-                for h in range(HIGHS):
-                    lhs.append(jnp.where(high == jnp.asarray(h, jnp.bfloat16), weight, zero))
-                rhs.append(jnp.where(low == low_mark, one, zero))
-            acc_ref[part] += lax.dot_general(
-                jnp.concatenate(lhs, axis=0), jnp.concatenate(rhs, axis=0),
-                (((1,), (1,)), ((), ())), preferred_element_type=jnp.float32,
-            )
-        return carry
-
-    lax.fori_loop(0, chunks_ref[0], chunk, 0)
-    wide = HIGHS * 16
-    for f in range(feats):
-        part, k = f // HIGHS, f % HIGHS
-        pieces = [
-            acc_ref[part, k * wide + h * 16 : k * wide + (h + 1) * 16, k * LOWS : (k + 1) * LOWS]
-            for h in range(HIGHS)
-        ]
-        hist_ref[f] = jnp.concatenate(pieces, axis=1).astype(jnp.bfloat16)
+    for g in range(GROUPS):
+
+        def chunk(t, carry, g=g):
+            at = pl.ds(pl.multiple_of((chunks_ref[g, 0] + t) * CHUNK, CHUNK), CHUNK)
+            weight = weight_ref[:, at].astype(jnp.bfloat16)
+            for first in range(0, feats, HIGHS):
+                lhs = []
+                rhs = [None] * HIGHS
+                for k in range(HIGHS):
+                    f = first + k
+                    high = jnp.broadcast_to(high_ref[f : f + 1, at], (16, CHUNK)).astype(jnp.bfloat16)
+                    low = jnp.broadcast_to(low_ref[f : f + 1, at], (LOWS, CHUNK)).astype(jnp.bfloat16)
+                    for j in range(wide // 16):
+                        marks = (slot + j * GROUPS).astype(jnp.float32).astype(jnp.bfloat16)
+                        lhs.append(jnp.where(high == marks, weight, zero))
+                    rhs[k // GROUPS * GROUPS + (k + g) % GROUPS] = jnp.where(low == low_mark, one, zero)
+                out = lax.dot_general(
+                    jnp.concatenate(lhs, axis=0), jnp.concatenate(rhs, axis=0),
+                    (((1,), (1,)), ((), ())), preferred_element_type=jnp.float32,
+                )
+                for k in range(HIGHS):
+                    half = k // GROUPS * 128
+                    mine = lane // LOWS == (k + g) % GROUPS
+                    acc_ref[first + k] += jnp.where(
+                        mine, out[k * wide : (k + 1) * wide, half : half + 128], 0.0
+                    )
+            return carry
+
+        lax.fori_loop(0, chunks_ref[g, 1], chunk, 0)
+    hist_ref[...] = acc_ref[...].astype(jnp.bfloat16)
 
 
 def histograms(smaller, counts, lam, row_child, bin_codes):
     query_dev, feat_dev, slots = bin_codes.shape
-    room = query_dev * slots + CHUNK
+    room = query_dev * slots + GROUPS * CHUNK + BLOCK + 256
+    vmem = pl.BlockSpec(memory_space=pltpu.VMEM)
     smem = pl.BlockSpec(memory_space=pltpu.SMEM)
-
-    def whole(array):
-        return pl.BlockSpec(array.shape, lambda i: (0,) * array.ndim, pipeline_mode=pl.Buffered(1))
-
+    wide = HIGHS * 16 // GROUPS
     return pl.pallas_call(
         histogram_kernel,
-        grid=(feat_dev // FEATS,),
-        out_shape=jax.ShapeDtypeStruct((feat_dev, 16, 256), jnp.bfloat16),
-        in_specs=[smem, smem, whole(lam), whole(row_child), whole(bin_codes)],
-        out_specs=pl.BlockSpec((FEATS, 16, 256), lambda i: (i, 0, 0)),
+        out_shape=jax.ShapeDtypeStruct((feat_dev, wide, 128), jnp.bfloat16),
+        in_specs=[smem, smem, vmem, vmem, vmem],
+        out_specs=vmem,
         scratch_shapes=[
             pltpu.VMEM((feat_dev, room), jnp.float32),
             pltpu.VMEM((feat_dev, room), jnp.float32),
             pltpu.VMEM((16, room), jnp.float32),
-            pltpu.VMEM((FEATS // HIGHS, HIGHS * HIGHS * 16, 256), jnp.float32),
-            pltpu.SMEM((1,), jnp.int32),
+            pltpu.VMEM((query_dev, feat_dev + 16, slots), jnp.bfloat16),
+            pltpu.VMEM((GROUPS, 8, slots), jnp.float32),
+            pltpu.VMEM((feat_dev, wide, 128), jnp.float32),
+            pltpu.SMEM((GROUPS, 2), jnp.int32),
         ],
         name="histograms",
     )(smaller, counts, lam, row_child, bin_codes)
 
 
 def gain_kernel(parts_ref, send_ref):
-    rows, bins = parts_ref.shape[1:]
-    built = jnp.sum(parts_ref[...].astype(jnp.float32), axis=0)
+    wide = HIGHS * 16 // GROUPS
+    feats = parts_ref.shape[1] // wide
+    bins = HIGHS * LOWS
+    kinds = 16 // GROUPS
+    summed = jnp.sum(parts_ref[...].astype(jnp.float32), axis=0)
+    built = []
+    for f in range(feats):
+        turn = (lax.axis_index("row") * feats + f) % GROUPS
+        block = pltpu.roll(summed[f * wide : (f + 1) * wide], (GROUPS - turn) * LOWS % 128, 1)
+        stats = ([], [])
+        for g in range(GROUPS):
+            pieces = [block[h * kinds : (h + 1) * kinds, g * LOWS : (g + 1) * LOWS] for h in range(HIGHS)]
+            both = jnp.concatenate(pieces, axis=1)
+            stats[0].append(both[: kinds // 2])
+            stats[1].append(both[kinds // 2 :])
+        built += stats[0] + stats[1]
+    built = jnp.concatenate(built, axis=0)
+    rows = built.shape[0]
     below = lax.broadcasted_iota(jnp.int32, (bins, bins), 0)
     upto = lax.broadcasted_iota(jnp.int32, (bins, bins), 1)
     left = jnp.dot(
@@ -268,7 +327,7 @@
     )
     threshold = lax.broadcasted_iota(jnp.int32, (8, bins), 1)
     best = jnp.full((8, 1), -jnp.inf, jnp.float32)
-    for f in range(rows // 16):
+    for f in range(feats):
         grad_left = left[f * 16 : f * 16 + 8]
         hess_left = left[f * 16 + 8 : f * 16 + 16]
         grad_total = grad_left[:, bins - 1 : bins]
@@ -328,7 +387,7 @@
     smem = pl.BlockSpec(memory_space=pltpu.SMEM)
     lam = lax.all_to_all(lambdas(scores, labels, counts), "feat", 0, 0, tiled=True)
     hist = histograms(smaller, counts, lam, row_child, bin_codes)
-    parts = lax.all_to_all(hist.reshape(row_count, rows, bins), "row", 0, 0, tiled=True)
+    parts = lax.all_to_all(hist.reshape(row_count, -1, 128), "row", 0, 0, tiled=True)
     send = pl.pallas_call(
         gain_kernel,
         out_shape=jax.ShapeDtypeStruct((row_count, bin_span, 128), jnp.float32),

time: 95.2 us -> 92.2 us (0.968)
  blocking collectives: 60.1 us -> 58.4 us
  Pallas kernels: 25.3 us -> 24 us
    all_to_all x1, blocking collectives: 31 us -> 29.2 us  [shards(): lax.all_to_all(hist.reshape(row_count, -1, 128), 'row', 0, 0, tiled=True)]
    pallas_call x1, Pallas kernels: 14.8 us -> 13.4 us  [histograms(): pl.pallas_call(histogram_kernel, out_shape=jax.ShapeDtypeStruct((feat_dev...]
where the time goes in v5:
time: 92.2 us; the launch traced here: 91.8 us
  blocking collectives  58.4 us (63%)
  Pallas kernels  24 us (26%)
  starting transfers between devices  5.93 us (6%)
  waiting for transfers between devices  1.6 us (2%)
  local copies, waits for them, and re-layouts  1.2 us (1%)
    all_to_all x1, blocking collectives, shards(): lax.all_to_all(hist.reshape(row_count, -1, 128), 'row', 0, 0, tiled=True)  29.2 us
    all_to_all x1, blocking collectives, shards(): own = lax.all_to_all(send, 'row', 0, 0, tiled=True)  17.3 us
    pallas_call x1, Pallas kernels, histograms(): pl.pallas_call(histogram_kernel, out_shape=jax.ShapeDtypeStruct((feat_dev...  13.4 us
    all_to_all x1, blocking collectives, shards(): lax.all_to_all(lambdas(scores, labels, counts), 'feat', 0, 0, tiled=True)  11.8 us
    all_to_all x1, starting transfers between devices, shards(): best = jnp.max(lax.all_to_all(best, 'feat', 0, 0, tiled=True), axis=0)  5.93 us
    pallas_call x1, Pallas kernels, lambdas(): pl.pallas_call(lambda_kernel, out_shape=jax.ShapeDtypeStruct((slots // SH...  4.96 us
    pallas_call x1, Pallas kernels, shards(): pl.pallas_call(children_kernel, out_shape=jax.ShapeDtypeStruct((bin_span,...  3.14 us
    pallas_call x1, Pallas kernels, shards(): pl.pallas_call(gain_kernel, out_shape=jax.ShapeDtypeStruct((row_count, bi...  2.48 us
  transfers between devices with their start and end apart: 1, of which 1 were waited for; matrix products, arithmetic and copies ran while one was open for 0% of the time, Pallas kernels for 3%

profile of v5, /device:TPU:1, one launch (start us, length us, event | category | flops | bytes accessed | tf_op | source)
XLA Modules:
  0.0 91.8 jit_solution(15966697928465274708)
XLA Ops:
  0.6 5.0 %lambdas.1 = bf16[8,16,128]{2,1,0:T(8,128)(2,1)} custom-call(s32[6]{0:T(128)} %counts_ref.3, f32[6,1024]{1,0:T(8,128)} %scores_ref.1, s32[6,1024]{1,0:T(8,128)} %labels_ref.1), custom_call_target="tpu_custom_call" | custom-call | tf_op jit(solution)/shard_map/lambdas/pallas_call | solution.py:98
  5.6 11.8 %all_to_all.20.lam_ref = bf16[8,16,128]{2,1,0:T(8,128)(2,1)} all-to-all(bf16[8,16,128]{2,1,0:T(8,128)(2,1)} %lambdas.1), channel_id=1, replica_groups=mesh['row'=32,'feat'=8] {'feat'}, dimensions={0} | all-to-all | bytes 65536 | tf_op jit(solution)/shard_map/all_to_all | solution.py:388
  17.4 13.4 %histograms.1 = bf16[96,32,128]{2,1,0:T(8,128)(2,1)} custom-call(s32[8]{0:T(128)} %smaller_ref.3, s32[6]{0:T(128)} %counts_ref.3, bf16[8,16,128]{2,1,0:T(8,128)(2,1)} %all_to_all.20.lam_ref, s32[6,1024]{1,0:T(8,128)} %child_ref.1, s32[6,96,1024]{2,1,0:T(8,128)} %codes_ref.1), custom_call_target="tpu_custom_call" | custom-call | tf_op jit(solution)/shard_map/histograms/pallas_call | solution.py:285
  30.8 29.2 %all_to_all.21.parts_ref = bf16[32,96,128]{2,1,0:T(8,128)(2,1)} all-to-all(bf16[32,96,128]{2,1,0:T(8,128)(2,1)} %bitcast.3), channel_id=1, replica_groups=mesh['row'=32,'feat'=8] {'row'}, dimensions={0} | all-to-all | bytes 1572864 | tf_op jit(solution)/shard_map/all_to_all | solution.py:390
  60.0 2.5 %gains.1 = f32[32,8,128]{2,1,0:T(8,128)} custom-call(bf16[32,96,128]{2,1,0:T(8,128)(2,1)} %all_to_all.21.parts_ref), custom_call_target="tpu_custom_call" | custom-call | tf_op jit(solution)/shard_map/gains/pallas_call | solution.py:391
  62.5 17.3 %all_to_all.22.parts_ref = f32[32,8,128]{2,1,0:T(8,128)S(1)} all-to-all(f32[32,8,128]{2,1,0:T(8,128)} %gains.1), channel_id=1, replica_groups=mesh['row'=32,'feat'=8] {'row'}, dimensions={0} | all-to-all | bytes 262144 | tf_op jit(solution)/shard_map/all_to_all | solution.py:396
  79.8 0.0 copy-start
  79.9 0.6 broadcast_in_dim.2
  80.5 5.9 %all-to-all-start.3 = ((f32[8,8,128]{2,1,0:T(8,128)}), f32[8,8,128]{2,1,0:T(8,128)S(1)}, u32[]{:S(2)}, u32[]{:S(2)}) async-start(f32[8,8,128]{2,1,0:T(8,128)} %broadcast_in_dim.2), calls=%async_computation.3 | async-start | bytes 65536 | tf_op jit(solution)/shard_map/all_to_all | solution.py:398
  86.4 0.0 copy-done
  86.4 3.1 %children.1 = f32[8,8,384]{2,1,0:T(8,128)} custom-call(s32[8]{0:T(128)} %smaller_ref.3, f32[32,8,128]{2,1,0:T(8,128)} %copy-done, f32[8,8,192]{2,1,0:T(8,128)} %parent_ref.1), custom_call_target="tpu_custom_call" | custom-call | tf_op jit(solution)/shard_map/children/pallas_call | solution.py:399
  89.6 1.6 %all-to-all-done.3 = f32[8,8,128]{2,1,0:T(8,128)S(1)} async-done(((f32[8,8,128]{2,1,0:T(8,128)}), f32[8,8,128]{2,1,0:T(8,128)S(1)}, u32[]{:S(2)}, u32[]{:S(2)}) %all-to-all-start.3) | async-done | bytes 32800 | tf_op jit(solution)/shard_map/all_to_all | solution.py:398
  91.2 0.6 slice_bitcast_fusion
  (2 shorter events, 0.0 us)
Async XLA Ops:
  79.8 6.6 %copy-start = (f32[32,8,128]{2,1,0:T(8,128)}, f32[32,8,128]{2,1,0:T(8,128)S(1)}, u32[]{:S(2)}) copy-start(f32[32,8,128]{2,1,0:T(8,128)S(1)} %all_to_all.22.parts_ref) | copy-start | bytes 393220
  80.5 10.7 %all-to-all-start.3 = ((f32[8,8,128]{2,1,0:T(8,128)}), f32[8,8,128]{2,1,0:T(8,128)S(1)}, u32[]{:S(2)}, u32[]{:S(2)}) async-start(f32[8,8,128]{2,1,0:T(8,128)} %broadcast_in_dim.2), calls=%async_computation.3 | async-start | bytes 65536 | tf_op jit(solution)/shard_map/all_to_all | solution.py:398

commit v6 on v5

--- a/solution.py
+++ b/solution.py
@@ -246,16 +246,16 @@
     acc_ref[...] = jnp.zeros_like(acc_ref)
     for g in range(GROUPS):
 
-        def chunk(t, carry, g=g):
-            at = pl.ds(pl.multiple_of((chunks_ref[g, 0] + t) * CHUNK, CHUNK), CHUNK)
+        def chunk(t, carry, g=g, size=CHUNK):
+            at = pl.ds(pl.multiple_of((chunks_ref[g, 0] + t) * CHUNK, CHUNK), size)
             weight = weight_ref[:, at].astype(jnp.bfloat16)
             for first in range(0, feats, HIGHS):
                 lhs = []
                 rhs = [None] * HIGHS
                 for k in range(HIGHS):
                     f = first + k
-                    high = jnp.broadcast_to(high_ref[f : f + 1, at], (16, CHUNK)).astype(jnp.bfloat16)
-                    low = jnp.broadcast_to(low_ref[f : f + 1, at], (LOWS, CHUNK)).astype(jnp.bfloat16)
+                    high = jnp.broadcast_to(high_ref[f : f + 1, at], (16, size)).astype(jnp.bfloat16)
+                    low = jnp.broadcast_to(low_ref[f : f + 1, at], (LOWS, size)).astype(jnp.bfloat16)
                     for j in range(wide // 16):
                         marks = (slot + j * GROUPS).astype(jnp.float32).astype(jnp.bfloat16)
                         lhs.append(jnp.where(high == marks, weight, zero))
@@ -272,7 +272,12 @@
                     )
             return carry
 
-        lax.fori_loop(0, chunks_ref[g, 1], chunk, 0)
+        def double(t, carry, chunk=chunk):
+            return chunk(2 * t, carry, size=2 * CHUNK)
+
+        pairs = chunks_ref[g, 1] // 2
+        lax.fori_loop(0, pairs, double, 0)
+        lax.fori_loop(2 * pairs, chunks_ref[g, 1], chunk, 0)
     hist_ref[...] = acc_ref[...].astype(jnp.bfloat16)
 
 
@@ -343,12 +348,14 @@
     stacked = jnp.concatenate(
         (built, jnp.broadcast_to(best, (8, bins)), jnp.zeros((128 - rows - 8, bins), jnp.float32)), axis=0
     )
-    send_ref[...] = stacked.T.reshape(send_ref.shape)
+    by_bin = stacked.T.reshape(send_ref.shape[0], -1, 128)
+    half = send_ref.shape[1]
+    send_ref[...] = jnp.concatenate((by_bin[:, :half, :64], by_bin[:, half:, :64]), axis=2)
 
 
 def children_kernel(smaller_ref, parts_ref, parent_ref, children_ref):
-    sources, bin_span, lanes = parts_ref.shape
-    parents, width = children_ref.shape[1:]
+    sources, half, lanes = parts_ref.shape
+    bin_span, parents, width = children_ref.shape
     group = width // sources
     column = lax.broadcasted_iota(jnp.int32, (sources, width), 1)
     source = lax.broadcasted_iota(jnp.int32, (sources, width), 0)
@@ -367,11 +374,15 @@
         precision=lax.Precision.HIGHEST, preferred_element_type=jnp.float32,
     )
     for b in range(bin_span):
-        wide = lax.dot_general(
-            parts_ref[:, b, :], spread, (((0,), (0,)), ((), ())),
-            precision=lax.Precision.HIGHEST, preferred_element_type=jnp.float32,
-        )
-        kept = jnp.where(match, wide[:rows], 0.0)
+        if b < half:
+            wide = lax.dot_general(
+                parts_ref[:, b, :], spread, (((0,), (0,)), ((), ())),
+                precision=lax.Precision.HIGHEST, preferred_element_type=jnp.float32,
+            )
+            later = (wide[64 : 64 + rows],) if b == 0 else later + (wide[64 : 64 + rows],)
+            kept = jnp.where(match, wide[:rows], 0.0)
+        else:
+            kept = jnp.where(match, later[b - half], 0.0)
         built = jnp.sum(kept.reshape(rows // parents, parents, width), axis=0)
         children_ref[b] = jnp.where(chosen, built, parent[b * parents : (b + 1) * parents] - built)
 
@@ -390,11 +401,11 @@
     parts = lax.all_to_all(hist.reshape(row_count, -1, 128), "row", 0, 0, tiled=True)
     send = pl.pallas_call(
         gain_kernel,
-        out_shape=jax.ShapeDtypeStruct((row_count, bin_span, 128), jnp.float32),
+        out_shape=jax.ShapeDtypeStruct((row_count, bin_span // 2, 128), jnp.float32),
         in_specs=[vmem], out_specs=vmem, name="gains",
     )(parts)
     own = lax.all_to_all(send, "row", 0, 0, tiled=True)
-    best = jnp.broadcast_to(jnp.max(own, axis=0)[None], (feat_count, bin_span, 128))
+    best = jnp.broadcast_to(jnp.max(own, axis=0)[None], (feat_count, bin_span // 2, 128))
     best = jnp.max(lax.all_to_all(best, "feat", 0, 0, tiled=True), axis=0)
     children = pl.pallas_call(
         children_kernel,

time: 92.2 us -> 91.2 us (0.989)
  Pallas kernels: 24 us -> 22.7 us
where the time goes in v6:
time: 91.2 us; the launch traced here: 90.7 us
  blocking collectives  58.2 us (64%)
  Pallas kernels  22.7 us (25%)
  starting transfers between devices  5.76 us (6%)
  waiting for transfers between devices  2.17 us (2%)
  local copies, waits for them, and re-layouts  1.19 us (1%)
    all_to_all x1, blocking collectives, shards(): lax.all_to_all(hist.reshape(row_count, -1, 128), 'row', 0, 0, tiled=True)  29.2 us
    all_to_all x1, blocking collectives, shards(): own = lax.all_to_all(send, 'row', 0, 0, tiled=True)  17.1 us
    pallas_call x1, Pallas kernels, histograms(): pl.pallas_call(histogram_kernel, out_shape=jax.ShapeDtypeStruct((feat_dev...  12.7 us
    all_to_all x1, blocking collectives, shards(): lax.all_to_all(lambdas(scores, labels, counts), 'feat', 0, 0, tiled=True)  11.8 us
    all_to_all x1, starting transfers between devices, shards(): best = jnp.max(lax.all_to_all(best, 'feat', 0, 0, tiled=True), axis=0)  5.76 us
    pallas_call x1, Pallas kernels, lambdas(): pl.pallas_call(lambda_kernel, out_shape=jax.ShapeDtypeStruct((slots // SH...  4.96 us
    pallas_call x1, Pallas kernels, shards(): pl.pallas_call(gain_kernel, out_shape=jax.ShapeDtypeStruct((row_count, bi...  2.55 us
    pallas_call x1, Pallas kernels, shards(): pl.pallas_call(children_kernel, out_shape=jax.ShapeDtypeStruct((bin_span,...  2.5 us
  transfers between devices with their start and end apart: 1, of which 1 were waited for; matrix products, arithmetic and copies ran while one was open for 0% of the time, Pallas kernels for 3%

profile of v6, /device:TPU:1, one launch (start us, length us, event | category | flops | bytes accessed | tf_op | source)
XLA Modules:
  0.0 90.7 jit_solution(15146646471666875950)
XLA Ops:
  0.6 5.0 %lambdas.1 = bf16[8,16,128]{2,1,0:T(8,128)(2,1)} custom-call(s32[6]{0:T(128)} %counts_ref.3, f32[6,1024]{1,0:T(8,128)} %scores_ref.1, s32[6,1024]{1,0:T(8,128)} %labels_ref.1), custom_call_target="tpu_custom_call" | custom-call | tf_op jit(solution)/shard_map/lambdas/pallas_call | solution.py:98
  5.6 11.8 %all_to_all.20.lam_ref = bf16[8,16,128]{2,1,0:T(8,128)(2,1)} all-to-all(bf16[8,16,128]{2,1,0:T(8,128)(2,1)} %lambdas.1), channel_id=1, replica_groups=mesh['row'=32,'feat'=8] {'feat'}, dimensions={0} | all-to-all | bytes 65536 | tf_op jit(solution)/shard_map/all_to_all | solution.py:399
  17.4 12.7 %histograms.1 = bf16[96,32,128]{2,1,0:T(8,128)(2,1)} custom-call(s32[8]{0:T(128)} %smaller_ref.3, s32[6]{0:T(128)} %counts_ref.3, bf16[8,16,128]{2,1,0:T(8,128)(2,1)} %all_to_all.20.lam_ref, s32[6,1024]{1,0:T(8,128)} %child_ref.1, s32[6,96,1024]{2,1,0:T(8,128)} %codes_ref.1), custom_call_target="tpu_custom_call" | custom-call | tf_op jit(solution)/shard_map/histograms/pallas_call | solution.py:290
  30.2 29.2 %all_to_all.21.parts_ref = bf16[32,96,128]{2,1,0:T(8,128)(2,1)} all-to-all(bf16[32,96,128]{2,1,0:T(8,128)(2,1)} %bitcast.3), channel_id=1, replica_groups=mesh['row'=32,'feat'=8] {'row'}, dimensions={0} | all-to-all | bytes 1572864 | tf_op jit(solution)/shard_map/all_to_all | solution.py:401
  59.4 2.5 %gains.1 = f32[32,4,128]{2,1,0:T(4,128)} custom-call(bf16[32,96,128]{2,1,0:T(8,128)(2,1)} %all_to_all.21.parts_ref), custom_call_target="tpu_custom_call" | custom-call | tf_op jit(solution)/shard_map/gains/pallas_call | solution.py:402
  62.0 17.1 %all_to_all.22.parts_ref = f32[32,4,128]{2,1,0:T(4,128)S(1)} all-to-all(f32[32,4,128]{2,1,0:T(4,128)} %gains.1), channel_id=1, replica_groups=mesh['row'=32,'feat'=8] {'row'}, dimensions={0} | all-to-all | bytes 131072 | tf_op jit(solution)/shard_map/all_to_all | solution.py:407
  79.0 0.0 copy-start
  79.1 0.6 broadcast_in_dim.2
  79.7 5.8 %all-to-all-start.3 = ((f32[8,4,128]{2,1,0:T(4,128)}), f32[8,4,128]{2,1,0:T(4,128)S(1)}, u32[]{:S(2)}, u32[]{:S(2)}) async-start(f32[8,4,128]{2,1,0:T(4,128)} %broadcast_in_dim.2), calls=%async_computation.3 | async-start | bytes 32768 | tf_op jit(solution)/shard_map/all_to_all | solution.py:409
  85.4 0.0 copy-done
  85.4 2.5 %children.1 = f32[8,8,384]{2,1,0:T(8,128)} custom-call(s32[8]{0:T(128)} %smaller_ref.3, f32[32,4,128]{2,1,0:T(4,128)} %copy-done, f32[8,8,192]{2,1,0:T(8,128)} %parent_ref.1), custom_call_target="tpu_custom_call" | custom-call | tf_op jit(solution)/shard_map/children/pallas_call | solution.py:410
  87.9 2.2 %all-to-all-done.3 = f32[8,4,128]{2,1,0:T(4,128)S(1)} async-done(((f32[8,4,128]{2,1,0:T(4,128)}), f32[8,4,128]{2,1,0:T(4,128)S(1)}, u32[]{:S(2)}, u32[]{:S(2)}) %all-to-all-start.3) | async-done | bytes 16416 | tf_op jit(solution)/shard_map/all_to_all | solution.py:409
  90.1 0.6 slice_bitcast_fusion
  (2 shorter events, 0.1 us)
Async XLA Ops:
  79.0 6.4 %copy-start = (f32[32,4,128]{2,1,0:T(4,128)}, f32[32,4,128]{2,1,0:T(4,128)S(1)}, u32[]{:S(2)}) copy-start(f32[32,4,128]{2,1,0:T(4,128)S(1)} %all_to_all.22.parts_ref) | copy-start | bytes 196612
  79.7 10.4 %all-to-all-start.3 = ((f32[8,4,128]{2,1,0:T(4,128)}), f32[8,4,128]{2,1,0:T(4,128)S(1)}, u32[]{:S(2)}, u32[]{:S(2)}) async-start(f32[8,4,128]{2,1,0:T(4,128)} %broadcast_in_dim.2), calls=%async_computation.3 | async-start | bytes 32768 | tf_op jit(solution)/shard_map/all_to_all | solution.py:409

commit v7 on v6

--- a/solution.py
+++ b/solution.py
@@ -14,6 +14,7 @@
 LOWS = 256 // HIGHS
 CHUNK = 256
 BLOCK = 512
+INNER = 8
 
 
 def node_column(smaller_ref, parents):
@@ -398,7 +399,16 @@
     smem = pl.BlockSpec(memory_space=pltpu.SMEM)
     lam = lax.all_to_all(lambdas(scores, labels, counts), "feat", 0, 0, tiled=True)
     hist = histograms(smaller, counts, lam, row_child, bin_codes)
-    parts = lax.all_to_all(hist.reshape(row_count, -1, 128), "row", 0, 0, tiled=True)
+    outer = row_count // INNER
+    across = [[x * INNER + z for x in range(outer)] for z in range(INNER)]
+    along = [[x * INNER + z for z in range(INNER)] for x in range(outer)]
+    parts = lax.all_to_all(
+        hist.reshape(outer, -1, 128), "row", 0, 0, axis_index_groups=across, tiled=True
+    )
+    parts = jnp.sum(parts.astype(jnp.float32), axis=0).astype(jnp.bfloat16)
+    parts = lax.all_to_all(
+        parts.reshape(INNER, -1, 128), "row", 0, 0, axis_index_groups=along, tiled=True
+    )
     send = pl.pallas_call(
         gain_kernel,
         out_shape=jax.ShapeDtypeStruct((row_count, bin_span // 2, 128), jnp.float32),

time: 91.2 us -> 89.8 us (0.985)
  blocking collectives: 58.2 us -> 55.8 us
  starting transfers between devices: 5.76 us -> 7.18 us
    all_to_all x1, blocking collectives: 17.1 us -> 13.1 us  [shards(): own = lax.all_to_all(send, 'row', 0, 0, tiled=True)]
    all_to_all x1 -> x2, blocking collectives: 29.2 us -> 30.8 us  [the longest x1 16 us: shards(): lax.all_to_all(parts.reshape(INNER, -1, 128), 'row', 0, 0, axis_index_gro...]
    all_to_all x1, starting transfers between devices: 5.76 us -> 7.18 us  [shards(): best = jnp.max(lax.all_to_all(best, 'feat', 0, 0, tiled=True), axis=0)]
where the time goes in v7:
time: 89.8 us; the launch traced here: 89 us
  blocking collectives  55.8 us (62%)
  Pallas kernels  21.8 us (24%)
  starting transfers between devices  7.18 us (8%)
  waiting for transfers between devices  2.17 us (2%)
  local copies, waits for them, and re-layouts  1.19 us (1%)
    all_to_all x1, blocking collectives, shards(): lax.all_to_all(parts.reshape(INNER, -1, 128), 'row', 0, 0, axis_index_gro...  16 us
    all_to_all x1, blocking collectives, shards(): lax.all_to_all(hist.reshape(outer, -1, 128), 'row', 0, 0, axis_index_grou...  14.8 us
    all_to_all x1, blocking collectives, shards(): own = lax.all_to_all(send, 'row', 0, 0, tiled=True)  13.1 us
    pallas_call x1, Pallas kernels, histograms(): pl.pallas_call(histogram_kernel, out_shape=jax.ShapeDtypeStruct((feat_dev...  12.1 us
    all_to_all x1, blocking collectives, shards(): lax.all_to_all(lambdas(scores, labels, counts), 'feat', 0, 0, tiled=True)  11.8 us
    all_to_all x1, starting transfers between devices, shards(): best = jnp.max(lax.all_to_all(best, 'feat', 0, 0, tiled=True), axis=0)  7.18 us
    pallas_call x1, Pallas kernels, lambdas(): pl.pallas_call(lambda_kernel, out_shape=jax.ShapeDtypeStruct((slots // SH...  4.96 us
    pallas_call x1, Pallas kernels, shards(): pl.pallas_call(children_kernel, out_shape=jax.ShapeDtypeStruct((bin_span,...  2.5 us
  transfers between devices with their start and end apart: 1, of which 1 were waited for; matrix products, arithmetic and copies ran while one was open for 0% of the time, Pallas kernels for 3%

profile of v7, /device:TPU:1, one launch (start us, length us, event | category | flops | bytes accessed | tf_op | source)
XLA Modules:
  0.0 89.0 jit_solution(4415440389258362713)
XLA Ops:
  0.6 5.0 %lambdas.1 = bf16[8,16,128]{2,1,0:T(8,128)(2,1)} custom-call(s32[6]{0:T(128)} %counts_ref.3, f32[6,1024]{1,0:T(8,128)} %scores_ref.1, s32[6,1024]{1,0:T(8,128)} %labels_ref.1), custom_call_target="tpu_custom_call" | custom-call | tf_op jit(solution)/shard_map/lambdas/pallas_call | solution.py:99
  5.6 11.8 %all_to_all.25.lam_ref = bf16[8,16,128]{2,1,0:T(8,128)(2,1)} all-to-all(bf16[8,16,128]{2,1,0:T(8,128)(2,1)} %lambdas.1), channel_id=1, replica_groups=mesh['row'=32,'feat'=8] {'feat'}, dimensions={0} | all-to-all | bytes 65536 | tf_op jit(solution)/shard_map/all_to_all | solution.py:400
  17.4 12.1 %histograms.1 = bf16[96,32,128]{2,1,0:T(8,128)(2,1)} custom-call(s32[8]{0:T(128)} %smaller_ref.3, s32[6]{0:T(128)} %counts_ref.3, bf16[8,16,128]{2,1,0:T(8,128)(2,1)} %all_to_all.25.lam_ref, s32[6,1024]{1,0:T(8,128)} %child_ref.1, s32[6,96,1024]{2,1,0:T(8,128)} %codes_ref.1), custom_call_target="tpu_custom_call" | custom-call | tf_op jit(solution)/shard_map/histograms/pallas_call | solution.py:291
  29.5 14.8 %all_to_all.26 = bf16[4,768,128]{2,1,0:T(8,128)(2,1)S(1)} all-to-all(bf16[4,768,128]{2,1,0:T(8,128)(2,1)} %bitcast.4), channel_id=1, replica_groups={{0,64,128,192},{8,72,136,200},{16,80,144,208},{24,88,152,216},{32,96,16..., dimensions={0} | all-to-all | bytes 1572864 | tf_op jit(solution)/shard_map/all_to_all | solution.py:405
  44.3 0.2 reduce_sum.12
  44.5 16.0 %all_to_all.27.parts_ref = bf16[8,96,128]{2,1,0:T(8,128)(2,1)} all-to-all(bf16[8,96,128]{2,1,0:T(8,128)(2,1)S(1)} %bitcast.5), channel_id=1, replica_groups={{0,8,16,24,32,40,48,56},{64,72,80,88,96,104,112,120},{128,136,144,152,1..., dimensions={0} | all-to-all | bytes 393216 | tf_op jit(solution)/shard_map/all_to_all | solution.py:409
  60.5 2.3 %gains.1 = f32[32,4,128]{2,1,0:T(4,128)} custom-call(bf16[8,96,128]{2,1,0:T(8,128)(2,1)} %all_to_all.27.parts_ref), custom_call_target="tpu_custom_call" | custom-call | tf_op jit(solution)/shard_map/gains/pallas_call | solution.py:412
  62.8 13.1 %all_to_all.28.parts_ref = f32[32,4,128]{2,1,0:T(4,128)S(1)} all-to-all(f32[32,4,128]{2,1,0:T(4,128)} %gains.1), channel_id=1, replica_groups=mesh['row'=32,'feat'=8] {'row'}, dimensions={0} | all-to-all | bytes 131072 | tf_op jit(solution)/shard_map/all_to_all | solution.py:417
  75.9 0.0 copy-start
  75.9 0.6 broadcast_in_dim.2
  76.6 7.2 %all-to-all-start.4 = ((f32[8,4,128]{2,1,0:T(4,128)}), f32[8,4,128]{2,1,0:T(4,128)S(1)}, u32[]{:S(2)}, u32[]{:S(2)}) async-start(f32[8,4,128]{2,1,0:T(4,128)} %broadcast_in_dim.2), calls=%async_computation.4 | async-start | bytes 32768 | tf_op jit(solution)/shard_map/all_to_all | solution.py:419
  83.7 0.0 copy-done
  83.7 2.5 %children.1 = f32[8,8,384]{2,1,0:T(8,128)} custom-call(s32[8]{0:T(128)} %smaller_ref.3, f32[32,4,128]{2,1,0:T(4,128)} %copy-done, f32[8,8,192]{2,1,0:T(8,128)} %parent_ref.1), custom_call_target="tpu_custom_call" | custom-call | tf_op jit(solution)/shard_map/children/pallas_call | solution.py:420
  86.2 2.2 %all-to-all-done.4 = f32[8,4,128]{2,1,0:T(4,128)S(1)} async-done(((f32[8,4,128]{2,1,0:T(4,128)}), f32[8,4,128]{2,1,0:T(4,128)S(1)}, u32[]{:S(2)}, u32[]{:S(2)}) %all-to-all-start.4) | async-done | bytes 16416 | tf_op jit(solution)/shard_map/all_to_all | solution.py:419
  88.4 0.6 slice_bitcast_fusion
  (2 shorter events, 0.1 us)
Async XLA Ops:
  75.9 7.8 %copy-start = (f32[32,4,128]{2,1,0:T(4,128)}, f32[32,4,128]{2,1,0:T(4,128)S(1)}, u32[]{:S(2)}) copy-start(f32[32,4,128]{2,1,0:T(4,128)S(1)} %all_to_all.28.parts_ref) | copy-start | bytes 196612
  76.6 11.9 %all-to-all-start.4 = ((f32[8,4,128]{2,1,0:T(4,128)}), f32[8,4,128]{2,1,0:T(4,128)S(1)}, u32[]{:S(2)}, u32[]{:S(2)}) async-start(f32[8,4,128]{2,1,0:T(4,128)} %broadcast_in_dim.2), calls=%async_computation.4 | async-start | bytes 32768 | tf_op jit(solution)/shard_map/all_to_all | solution.py:419

commit v8 on v7

--- a/solution.py
+++ b/solution.py
@@ -360,7 +360,9 @@
     group = width // sources
     column = lax.broadcasted_iota(jnp.int32, (sources, width), 1)
     source = lax.broadcasted_iota(jnp.int32, (sources, width), 0)
-    spread = (column // group == source).astype(jnp.float32)
+    outer = sources // INNER
+    sender = (source % outer) * INNER + source // outer
+    spread = (column // group == sender).astype(jnp.float32)
     rows = group * parents // 2
     row = lax.broadcasted_iota(jnp.int32, (rows, width), 0)
     col = lax.broadcasted_iota(jnp.int32, (rows, width), 1)
@@ -414,7 +416,12 @@
         out_shape=jax.ShapeDtypeStruct((row_count, bin_span // 2, 128), jnp.float32),
         in_specs=[vmem], out_specs=vmem, name="gains",
     )(parts)
-    own = lax.all_to_all(send, "row", 0, 0, tiled=True)
+    own = lax.all_to_all(
+        send.reshape(outer, INNER, bin_span // 2, 128), "row", 0, 0, axis_index_groups=across, tiled=True
+    )
+    own = lax.all_to_all(
+        jnp.transpose(own, (1, 0, 2, 3)), "row", 0, 0, axis_index_groups=along, tiled=True
+    ).reshape(row_count, bin_span // 2, 128)
     best = jnp.broadcast_to(jnp.max(own, axis=0)[None], (feat_count, bin_span // 2, 128))
     best = jnp.max(lax.all_to_all(best, "feat", 0, 0, tiled=True), axis=0)
     children = pl.pallas_call(

time: 89.8 us -> 96.3 us (1.072)
  blocking collectives: 55.8 us -> 60.7 us
  starting transfers between devices: 7.18 us -> 8.75 us
    all_to_all x1 -> x2, blocking collectives: 13.1 us -> 17.3 us  [the longest x1 9.6 us: shards(): lax.all_to_all(jnp.transpose(own, (1, 0, 2, 3)), 'row', 0, 0, axis_index_...]
    all_to_all x1, starting transfers between devices: 7.18 us -> 8.75 us  [shards(): best = jnp.max(lax.all_to_all(best, 'feat', 0, 0, tiled=True), axis=0)]
where the time goes in v8:
time: 96.3 us; the launch traced here: 96.2 us
  blocking collectives  60.7 us (63%)
  Pallas kernels  22.5 us (23%)
  starting transfers between devices  8.75 us (9%)
  waiting for transfers between devices  2.17 us (2%)
  local copies, waits for them, and re-layouts  1.2 us (1%)
    all_to_all x1, blocking collectives, shards(): lax.all_to_all(parts.reshape(INNER, -1, 128), 'row', 0, 0, axis_index_gro...  16.7 us
    all_to_all x1, blocking collectives, shards(): lax.all_to_all(hist.reshape(outer, -1, 128), 'row', 0, 0, axis_index_grou...  14.8 us
    pallas_call x1, Pallas kernels, histograms(): pl.pallas_call(histogram_kernel, out_shape=jax.ShapeDtypeStruct((feat_dev...  12.7 us
    all_to_all x1, blocking collectives, shards(): lax.all_to_all(lambdas(scores, labels, counts), 'feat', 0, 0, tiled=True)  11.8 us
    all_to_all x1, blocking collectives, shards(): lax.all_to_all(jnp.transpose(own, (1, 0, 2, 3)), 'row', 0, 0, axis_index_...  9.6 us
    all_to_all x1, starting transfers between devices, shards(): best = jnp.max(lax.all_to_all(best, 'feat', 0, 0, tiled=True), axis=0)  8.75 us
    all_to_all x1, blocking collectives, shards(): lax.all_to_all(send.reshape(outer, INNER, bin_span // 2, 128), 'row', 0,...  7.73 us
    pallas_call x1, Pallas kernels, lambdas(): pl.pallas_call(lambda_kernel, out_shape=jax.ShapeDtypeStruct((slots // SH...  4.96 us
  transfers between devices with their start and end apart: 1, of which 1 were waited for; matrix products, arithmetic and copies ran while one was open for 0% of the time, Pallas kernels for 3%

profile of v8, /device:TPU:1, one launch (start us, length us, event | category | flops | bytes accessed | tf_op | source)
XLA Modules:
  0.0 96.2 jit_solution(6729775606396917685)
XLA Ops:
  0.6 5.0 %lambdas.1 = bf16[8,16,128]{2,1,0:T(8,128)(2,1)} custom-call(s32[6]{0:T(128)} %counts_ref.3, f32[6,1024]{1,0:T(8,128)} %scores_ref.1, s32[6,1024]{1,0:T(8,128)} %labels_ref.1), custom_call_target="tpu_custom_call" | custom-call | tf_op jit(solution)/shard_map/lambdas/pallas_call | solution.py:99
  5.6 11.8 %all_to_all.30.lam_ref = bf16[8,16,128]{2,1,0:T(8,128)(2,1)} all-to-all(bf16[8,16,128]{2,1,0:T(8,128)(2,1)} %lambdas.1), channel_id=1, replica_groups=mesh['row'=32,'feat'=8] {'feat'}, dimensions={0} | all-to-all | bytes 65536 | tf_op jit(solution)/shard_map/all_to_all | solution.py:402
  17.4 12.7 %histograms.1 = bf16[96,32,128]{2,1,0:T(8,128)(2,1)} custom-call(s32[8]{0:T(128)} %smaller_ref.3, s32[6]{0:T(128)} %counts_ref.3, bf16[8,16,128]{2,1,0:T(8,128)(2,1)} %all_to_all.30.lam_ref, s32[6,1024]{1,0:T(8,128)} %child_ref.1, s32[6,96,1024]{2,1,0:T(8,128)} %codes_ref.1), custom_call_target="tpu_custom_call" | custom-call | tf_op jit(solution)/shard_map/histograms/pallas_call | solution.py:291
  30.2 14.8 %all_to_all.31 = bf16[4,768,128]{2,1,0:T(8,128)(2,1)S(1)} all-to-all(bf16[4,768,128]{2,1,0:T(8,128)(2,1)} %bitcast.7), channel_id=1, replica_groups={{0,64,128,192},{8,72,136,200},{16,80,144,208},{24,88,152,216},{32,96,16..., dimensions={0} | all-to-all | bytes 1572864 | tf_op jit(solution)/shard_map/all_to_all | solution.py:407
  45.0 0.2 reduce_sum.12
  45.2 16.7 %all_to_all.32.parts_ref = bf16[8,96,128]{2,1,0:T(8,128)(2,1)} all-to-all(bf16[8,96,128]{2,1,0:T(8,128)(2,1)S(1)} %bitcast.8), channel_id=1, replica_groups={{0,8,16,24,32,40,48,56},{64,72,80,88,96,104,112,120},{128,136,144,152,1..., dimensions={0} | all-to-all | bytes 393216 | tf_op jit(solution)/shard_map/all_to_all | solution.py:411
  61.9 2.3 %gains.1 = f32[32,4,128]{2,1,0:T(4,128)} custom-call(bf16[8,96,128]{2,1,0:T(8,128)(2,1)} %all_to_all.32.parts_ref), custom_call_target="tpu_custom_call" | custom-call | tf_op jit(solution)/shard_map/gains/pallas_call | solution.py:414
  64.2 7.7 %all_to_all.33 = f32[4,8,4,128]{3,2,1,0:T(4,128)S(1)} all-to-all(f32[4,8,4,128]{3,2,1,0:T(4,128)} %bitcast.11), channel_id=1, replica_groups={{0,64,128,192},{8,72,136,200},{16,80,144,208},{24,88,152,216},{32,96,16..., dimensions={0} | all-to-all | bytes 131072 | tf_op jit(solution)/shard_map/all_to_all | solution.py:419
  71.9 9.6 %all_to_all.34 = f32[8,4,4,128]{3,2,1,0:T(4,128)S(1)} all-to-all(f32[8,4,4,128]{3,2,1,0:T(4,128)S(1)} %copy.13), channel_id=1, replica_groups={{0,8,16,24,32,40,48,56},{64,72,80,88,96,104,112,120},{128,136,144,152,1..., dimensions={0} | all-to-all | bytes 131072 | tf_op jit(solution)/shard_map/all_to_all | solution.py:422
  81.5 0.0 copy-start
  81.6 0.6 broadcast_in_dim.2
  82.2 8.7 %all-to-all-start.5 = ((f32[8,4,128]{2,1,0:T(4,128)}), f32[8,4,128]{2,1,0:T(4,128)S(1)}, u32[]{:S(2)}, u32[]{:S(2)}) async-start(f32[8,4,128]{2,1,0:T(4,128)} %broadcast_in_dim.2), calls=%async_computation.5 | async-start | bytes 32768 | tf_op jit(solution)/shard_map/all_to_all | solution.py:426
  90.9 0.0 copy-done
  90.9 2.5 %children.1 = f32[8,8,384]{2,1,0:T(8,128)} custom-call(s32[8]{0:T(128)} %smaller_ref.3, f32[32,4,128]{2,1,0:T(4,128)} %bitcast.9, f32[8,8,192]{2,1,0:T(8,128)} %parent_ref.1), custom_call_target="tpu_custom_call" | custom-call | tf_op jit(solution)/shard_map/children/pallas_call | solution.py:427
  93.4 2.2 %all-to-all-done.5 = f32[8,4,128]{2,1,0:T(4,128)S(1)} async-done(((f32[8,4,128]{2,1,0:T(4,128)}), f32[8,4,128]{2,1,0:T(4,128)S(1)}, u32[]{:S(2)}, u32[]{:S(2)}) %all-to-all-start.5) | async-done | bytes 16416 | tf_op jit(solution)/shard_map/all_to_all | solution.py:426
  95.6 0.6 slice_bitcast_fusion
  (3 shorter events, 0.1 us)
Async XLA Ops:
  81.5 9.4 %copy-start = (f32[8,4,4,128]{3,2,1,0:T(4,128)}, f32[8,4,4,128]{3,2,1,0:T(4,128)S(1)}, u32[]{:S(2)}) copy-start(f32[8,4,4,128]{3,2,1,0:T(4,128)S(1)} %all_to_all.34) | copy-start | bytes 196612
  82.2 13.4 %all-to-all-start.5 = ((f32[8,4,128]{2,1,0:T(4,128)}), f32[8,4,128]{2,1,0:T(4,128)S(1)}, u32[]{:S(2)}, u32[]{:S(2)}) async-start(f32[8,4,128]{2,1,0:T(4,128)} %broadcast_in_dim.2), calls=%async_computation.5 | async-start | bytes 32768 | tf_op jit(solution)/shard_map/all_to_all | solution.py:426
